TPU v7x, 512 devices: a whole 4x8x8 slice. The times are simulated.
512 devices in a mesh: tm: 64 (over y, z), head: 8 (over x, core).
Axes of the slice: x: 4, y: 8, z: 8, core: 2. Of those that a mesh axis runs over, the one named last changes fastest.
Arguments:
- queries: bfloat16 [16384, 3072], P('tm', 'head'), may hold values from -6 to 6
- keys: bfloat16 [8192, 3072], P('tm', 'head'), may hold values from -6 to 6
- values: bfloat16 [8192, 3072], P('tm', 'head'), may hold values from -6 to 6
- out_weight: bfloat16 [3072, 3072], P('head'), may hold values from -0.109375 to 0.109375
- out_grad: bfloat16 [16384, 3072], P('tm', 'head'), may hold values from -6 to 6
- align_lists: int32 [64, 4], replicated, may hold values from -1 to 63, as said below
- block_masks: int32 [128, 3], P('tm'), may hold values from -1 to 3, as said below
Outputs:
- mixed: bfloat16 [16384, 3072], P('tm', 'head')
- query_grad: bfloat16 [16384, 3072], P('tm', 'head')
- key_grad: bfloat16 [8192, 3072], P('tm', 'head')
- value_grad: bfloat16 [8192, 3072], P('tm', 'head')
Inputs may be any that keep to these rules, and one draw needn't show every extreme that they name: `align_lists`: row t holds a band of consecutive audio tile indices in its first slots and -1 in the rest; every listed tile a satisfies (t - 3) <= a < (t + 4). Some slab uses all 4 slots starting at (t - 3), and some slab's band ends at (t + 4) - 1. `block_masks`: row i names one or more consecutive used slots of the list of slab i // 2 in its first entries and -1 in the rest; some row has all 3 entries live.
All inputs are finite; a program needn't handle non-finite values.
Results may differ from a plain program's by a relative error of at most 0.025.
Values may be sent and summed in bfloat16 or wider, within the bound.
No kernel may reach another device: no remote copies, remote signals or barrier semaphores. Data moves between devices by JAX's collectives and lax.ppermute only.
A program may use at most 64 MiB of HBM per device.

v0:
```python
import math

import jax
import jax.numpy as jnp
from jax import lax
from jax.sharding import PartitionSpec as P

HEAD_DIM = 128
TILE = 128
BLOCKS = 3
REACH = 3


def from_behind(shard, axis, by):
    count = lax.axis_size(axis)
    pairs = [(i, i + by) for i in range(count) if 0 <= i + by < count]
    return lax.ppermute(shard, axis, pairs)


def local(queries, keys, values, out_weight, out_grad, align_lists, block_masks):
    slab_index = lax.axis_index("tm")
    video_rows, head_cols = queries.shape
    video_tiles = block_masks.shape[0]
    own_tiles = keys.shape[0] // TILE
    heads_here = head_cols // HEAD_DIM
    span_tiles = (2 * REACH + 1) * own_tiles
    score_scale = 1.0 / math.sqrt(HEAD_DIM)
    stacked = jnp.stack([keys, values], 0)
    fetched = []
    for offset in range(-REACH, REACH + 1):
        if offset == 0:
            fetched.append(stacked)
        else:
            fetched.append(from_behind(stacked, "tm", -offset))
    region = jnp.concatenate(fetched, 1).reshape(2, span_tiles, TILE, head_cols)
    list_row = lax.dynamic_index_in_dim(align_lists, slab_index, 0, keepdims=False)
    live_block = block_masks >= 0
    picked_tile = jnp.take(list_row, jnp.maximum(block_masks, 0), axis=0)
    local_tile = jnp.where(live_block, picked_tile - (slab_index - REACH) * own_tiles, 0)
    chosen = jnp.take(region, local_tile, axis=1)
    key_view = chosen[0].reshape(video_tiles, BLOCKS * TILE, heads_here, HEAD_DIM)
    value_view = chosen[1].reshape(video_tiles, BLOCKS * TILE, heads_here, HEAD_DIM)
    query_view = queries.reshape(video_tiles, TILE, heads_here, HEAD_DIM)
    scores = (
        jnp.einsum("vqhd,vkhd->vhqk", query_view, key_view, preferred_element_type=jnp.float32)
        * score_scale
    )
    key_live = jnp.repeat(live_block, TILE, axis=1)
    scores = jnp.where(key_live[:, None, None, :], scores, -jnp.inf)
    row_top = jnp.max(scores, -1, keepdims=True)
    exp_scores = jnp.exp(scores - row_top)
    soft_probs = exp_scores / jnp.sum(exp_scores, -1, keepdims=True)
    weights = soft_probs.astype(jnp.bfloat16)
    attended_view = jnp.einsum(
        "vhqk,vkhd->vqhd", weights, value_view, preferred_element_type=jnp.float32
    ).astype(jnp.bfloat16)
    attended = attended_view.reshape(video_rows, head_cols)
    partial_sum = jnp.dot(attended, out_weight, preferred_element_type=jnp.float32)
    mixed = lax.psum_scatter(
        partial_sum.astype(jnp.bfloat16), "head", scatter_dimension=1, tiled=True
    )
    grad_attended = lax.dot_general(
        lax.all_gather(out_grad, "head", axis=1, tiled=True),
        out_weight,
        (((1,), (1,)), ((), ())),
        preferred_element_type=jnp.float32,
    ).astype(jnp.bfloat16)
    grad_view = grad_attended.reshape(video_tiles, TILE, heads_here, HEAD_DIM)
    row_delta = jnp.sum(grad_view.astype(jnp.float32) * attended_view.astype(jnp.float32), -1)
    grad_probs = jnp.einsum(
        "vqhd,vkhd->vhqk", grad_view, value_view, preferred_element_type=jnp.float32
    )
    grad_scores = (
        soft_probs * (grad_probs - jnp.transpose(row_delta, (0, 2, 1))[..., None])
    ).astype(jnp.bfloat16)
    query_grad = (
        jnp.einsum("vhqk,vkhd->vqhd", grad_scores, key_view, preferred_element_type=jnp.float32)
        * score_scale
    )
    query_grad = query_grad.astype(jnp.bfloat16).reshape(video_rows, head_cols)
    key_terms = (
        jnp.einsum("vhqk,vqhd->vkhd", grad_scores, query_view, preferred_element_type=jnp.float32)
        * score_scale
    )
    value_terms = jnp.einsum(
        "vhqk,vqhd->vkhd", weights, grad_view, preferred_element_type=jnp.float32
    )
    term_stack = jnp.stack(
        [
            key_terms.reshape(video_tiles * BLOCKS, TILE, head_cols),
            value_terms.reshape(video_tiles * BLOCKS, TILE, head_cols),
        ],
        0,
    )
    onehot = (
        local_tile.reshape(-1)[:, None] == jnp.arange(span_tiles)[None, :]
    ) & live_block.reshape(-1)[:, None]
    sums_by_tile = jnp.einsum(
        "bn,sbtc->sntc", onehot.astype(jnp.float32), term_stack, precision=lax.Precision.HIGHEST
    )

    def owner_part(offset):
        low_tile = (offset + REACH) * own_tiles
        block = lax.slice_in_dim(sums_by_tile, low_tile, low_tile + own_tiles, axis=1)
        return block.reshape(2, own_tiles * TILE, head_cols)

    collected = owner_part(0)
    for offset in range(-REACH, REACH + 1):
        if offset != 0:
            collected = collected + from_behind(owner_part(offset), "tm", offset)
    key_grad = collected[0].astype(jnp.bfloat16)
    value_grad = collected[1].astype(jnp.bfloat16)
    return (mixed, query_grad, key_grad, value_grad)


def solution(mesh):
    return jax.shard_map(
        local,
        mesh=mesh,
        in_specs=(
            P("tm", "head"),
            P("tm", "head"),
            P("tm", "head"),
            P("head", None),
            P("tm", "head"),
            P(),
            P("tm", None),
        ),
        out_specs=(P("tm", "head"), P("tm", "head"), P("tm", "head"), P("tm", "head")),
        check_vma=False,
    )
```

profile of v0, /device:TPU:91, one launch (start us, length us, event | category | flops | bytes accessed | tf_op | source)
XLA Modules:
  0.0 211.6 jit_solution(15819606893248489810)
XLA Ops:
  8.4 9.6 %collective-permute-start.5 = (bf16[2,128,384]{2,1,0:T(8,128)(2,1)S(1)}, bf16[2,128,384]{2,1,0:T(8,128)(2,1)S(1)}, u32[]{:S(2)}, u32[]{:S(2)}) collective-permute-start(bf16[2,128,384]{2,1,0:T(8,128)(2,1)S(1)} %pad_maximum_fusion), channel_id=1, source_target_pairs={{24,0},{32,8},{40,16},{48,24},{56,32},{64,40},{72,48},{80,56},{88,... | collective-permute-start | bytes 589832 | tf_op jit(solution)/shard_map/ppermute | solution.py:17
  18.0 2.2 %collective-permute-start.4 = (bf16[2,128,384]{2,1,0:T(8,128)(2,1)S(1)}, bf16[2,128,384]{2,1,0:T(8,128)(2,1)S(1)}, u32[]{:S(2)}, u32[]{:S(2)}) collective-permute-start(bf16[2,128,384]{2,1,0:T(8,128)(2,1)S(1)} %pad_maximum_fusion), channel_id=1, source_target_pairs={{16,0},{24,8},{32,16},{40,24},{48,32},{56,40},{64,48},{72,56},{80,... | collective-permute-start | bytes 589832 | tf_op jit(solution)/shard_map/ppermute | solution.py:17
  22.1 4.3 %collective-permute-start.1 = (bf16[2,128,384]{2,1,0:T(8,128)(2,1)S(1)}, bf16[2,128,384]{2,1,0:T(8,128)(2,1)}, u32[]{:S(2)}, u32[]{:S(2)}) collective-permute-start(bf16[2,128,384]{2,1,0:T(8,128)(2,1)S(1)} %pad_maximum_fusion), channel_id=1, source_target_pairs={{0,16},{8,24},{16,32},{24,40},{32,48},{40,56},{48,64},{56,72},{64,... | collective-permute-start | bytes 589832 | tf_op jit(solution)/shard_map/ppermute | solution.py:17
  26.4 4.0 %collective-permute-start = (bf16[2,128,384]{2,1,0:T(8,128)(2,1)S(1)}, bf16[2,128,384]{2,1,0:T(8,128)(2,1)}, u32[]{:S(2)}, u32[]{:S(2)}) collective-permute-start(bf16[2,128,384]{2,1,0:T(8,128)(2,1)S(1)} %pad_maximum_fusion), channel_id=1, source_target_pairs={{0,24},{8,32},{16,40},{24,48},{32,56},{40,64},{48,72},{56,80},{64,... | collective-permute-start | bytes 589832 | tf_op jit(solution)/shard_map/ppermute | solution.py:17
  36.2 13.5 %collective-permute-done = bf16[2,128,384]{2,1,0:T(8,128)(2,1)} collective-permute-done((bf16[2,128,384]{2,1,0:T(8,128)(2,1)S(1)}, bf16[2,128,384]{2,1,0:T(8,128)(2,1)}, u32[]{:S(2)}, u32[]{:S(2)}) %collective-permute-start) | collective-permute-done | bytes 196640 | tf_op jit(solution)/shard_map/ppermute | solution.py:17
  53.9 2.8 %collective-permute-done.2 = bf16[2,128,384]{2,1,0:T(8,128)(2,1)S(1)} collective-permute-done((bf16[2,128,384]{2,1,0:T(8,128)(2,1)S(1)}, bf16[2,128,384]{2,1,0:T(8,128)(2,1)S(1)}, u32[]{:S(2)}, u32[]{:S(2)}) %collective-permute-start.2) | collective-permute-done | bytes 196640 | tf_op jit(solution)/shard_map/ppermute | solution.py:17
  64.7 2.7 %reshape_squeeze.6 = bf16[2,384,3,128]{3,2,1,0:T(4,128)(2,1)} reshape(bf16[1,2,3,128,384]{4,3,0,2,1:T(8,128)(2,1)} %get-tuple-element.23) | data formatting | bytes 1179648 | tf_op jit(solution)/shard_map/reshape;squeeze | solution.py:42
  69.0 3.1 %convolution_convert_fusion.1 = bf16[256,384]{1,0:T(8,128)(2,1)} fusion(bf16[256,3072]{1,0:T(8,128)(2,1)} %all-gather.2.cloned.1.call-done, bf16[384,3072]{1,0:T(8,128)(2,1)S(1)} %copy-done), kind=kOutput, calls=%fused_computation.22 | convolution fusion | flops 604078080 | bytes 4128768 | tf_op jit(solution)/shard_map/dot_general | solution.py:62
  73.9 2.8 %multiply_reduce_fusion = (f32[2,128,3]{1,2,0:T(4,128)S(1)}, bf16[2,128,3,128]{1,3,2,0:T(8,128)(2,1)}) fusion(bf16[2,128,3,128]{1,3,2,0:T(8,128)(2,1)} %copy.63, f32[2,3,128]{2,1,0:T(4,128)S(1)} %get-tuple-element.26, bf16[2,384,3,128]{1,3,2,0:T(8,128)(2,1)S(1)} %copy-done.2, pred[2,384]{1,0:T(4,128)(4,1)S(1)} %bitcast.133, ...), kind=kOutput, calls=%fused_computation.45 | convolution fusion | flops 152961408 | bytes 1776384 | tf_op jit(solution)/shard_map/vhqk,vkhd->vqhd/dot_general | solution.py:54
  80.0 2.6 %copy.88 = bf16[256,3072]{0,1:T(8,128)(2,1)} copy(bf16[256,3072]{1,0:T(8,128)(2,1)} %convolution_convert_fusion) | data formatting | bytes 3145728
  85.4 3.4 %copy.72 = f32[2,384,3,128]{1,0,3,2:T(2,128)} copy(f32[2,384,3,128]{1,3,2,0:T(8,128)} %convolution_bitcast_fusion) | data formatting | bytes 2359296 | tf_op jit(solution)/shard_map/vhqk,vqhd->vkhd/transpose | solution.py:85
  92.2 3.1 %stack_reshape.6 = f32[1,6,128,384]{2,1,3,0:T(8,128)} reshape(f32[2,384,3,128]{1,0,3,2:T(2,128)} %copy.69) | data formatting | bytes 2359296 | tf_op jit(solution)/shard_map/stack;reshape | solution.py:88
  95.2 3.1 %copy.73 = f32[1,6,128,384]{3,1,2,0:T(8,128)} copy(f32[1,6,128,384]{2,1,3,0:T(8,128)} %stack_reshape.6) | data formatting | bytes 2359296 | tf_op jit(solution)/shard_map/stack;reshape | solution.py:88
  100.5 3.1 %copy.74 = f32[1,6,128,384]{3,1,2,0:T(8,128)} copy(f32[1,6,128,384]{2,1,3,0:T(8,128)} %stack_reshape.7) | data formatting | bytes 2359296 | tf_op jit(solution)/shard_map/stack;reshape | solution.py:88
  103.6 3.7 %fusion.5 = f32[2,7,128,384]{3,1,2,0:T(8,128)S(1)} fusion(f32[1,6,128,384]{3,1,2,0:T(8,128)} %copy.74, f32[1,6,128,384]{3,1,2,0:T(8,128)} %copy.73, s32[6]{0:T(128)S(1)} %copy-done.17, pred[6]{0:T(512)(128)(4,1)S(1)} %copy-done.18), kind=kOutput, calls=%fused_computation.8 | convolution fusion | flops 50135124 | bytes 5111838 | tf_op jit(solution)/shard_map/bn,sbtc->sntc/dot_general | solution.py:98
  109.5 3.2 %collective-permute-start.10 = (f32[2,128,384]{2,1,0:T(8,128)S(1)}, f32[2,128,384]{2,1,0:T(8,128)S(1)}, u32[]{:S(2)}, u32[]{:S(2)}) collective-permute-start(f32[2,128,384]{2,1,0:T(8,128)S(1)} %bitcast.125), channel_id=1, source_target_pairs={{0,16},{8,24},{16,32},{24,40},{32,48},{40,56},{48,64},{56,72},{64,... | collective-permute-start | bytes 1179656 | tf_op jit(solution)/shard_map/ppermute | solution.py:17
  116.6 4.9 %collective-permute-start.11 = (f32[2,128,384]{2,1,0:T(8,128)}, f32[2,128,384]{2,1,0:T(8,128)}, u32[]{:S(2)}, u32[]{:S(2)}) collective-permute-start(f32[2,128,384]{2,1,0:T(8,128)} %bitcast.117), channel_id=1, source_target_pairs={{0,24},{8,32},{16,40},{24,48},{32,56},{40,64},{48,72},{56,80},{64,... | collective-permute-start | bytes 1179656 | tf_op jit(solution)/shard_map/ppermute | solution.py:17
  121.6 4.3 %collective-permute-start.6 = (f32[2,128,384]{2,1,0:T(8,128)}, f32[2,128,384]{2,1,0:T(8,128)}, u32[]{:S(2)}, u32[]{:S(2)}) collective-permute-start(f32[2,128,384]{2,1,0:T(8,128)} %bitcast.116), channel_id=1, source_target_pairs={{24,0},{32,8},{40,16},{48,24},{56,32},{64,40},{72,48},{80,56},{88,... | collective-permute-start | bytes 1179656 | tf_op jit(solution)/shard_map/ppermute | solution.py:17
  125.8 4.0 %collective-permute-start.7 = (f32[2,128,384]{2,1,0:T(8,128)}, f32[2,128,384]{2,1,0:T(8,128)}, u32[]{:S(2)}, u32[]{:S(2)}) collective-permute-start(f32[2,128,384]{2,1,0:T(8,128)} %bitcast.115), channel_id=1, source_target_pairs={{16,0},{24,8},{32,16},{40,24},{48,32},{56,40},{64,48},{72,56},{80,... | collective-permute-start | bytes 1179656 | tf_op jit(solution)/shard_map/ppermute | solution.py:17
  134.3 3.1 %collective-permute-start.9 = (f32[2,128,384]{2,1,0:T(8,128)}, f32[2,128,384]{2,1,0:T(8,128)}, u32[]{:S(2)}, u32[]{:S(2)}) collective-permute-start(f32[2,128,384]{2,1,0:T(8,128)} %bitcast.113), channel_id=1, source_target_pairs={{0,8},{8,16},{16,24},{24,32},{32,40},{40,48},{48,56},{56,64},{64,7... | collective-permute-start | bytes 1179656 | tf_op jit(solution)/shard_map/ppermute | solution.py:17
  138.7 14.9 %collective-permute-done.11 = f32[2,128,384]{2,1,0:T(8,128)} collective-permute-done((f32[2,128,384]{2,1,0:T(8,128)}, f32[2,128,384]{2,1,0:T(8,128)}, u32[]{:S(2)}, u32[]{:S(2)}) %collective-permute-start.11) | collective-permute-done | bytes 393248 | tf_op jit(solution)/shard_map/ppermute | solution.py:17
  153.5 11.3 %collective-permute-done.6 = f32[2,128,384]{2,1,0:T(8,128)} collective-permute-done((f32[2,128,384]{2,1,0:T(8,128)}, f32[2,128,384]{2,1,0:T(8,128)}, u32[]{:S(2)}, u32[]{:S(2)}) %collective-permute-start.6) | collective-permute-done | bytes 393248 | tf_op jit(solution)/shard_map/ppermute | solution.py:17
  164.9 19.4 %collective-permute-done.7 = f32[2,128,384]{2,1,0:T(8,128)} collective-permute-done((f32[2,128,384]{2,1,0:T(8,128)}, f32[2,128,384]{2,1,0:T(8,128)}, u32[]{:S(2)}, u32[]{:S(2)}) %collective-permute-start.7) | collective-permute-done | bytes 393248 | tf_op jit(solution)/shard_map/ppermute | solution.py:17
  184.3 16.3 %collective-permute-done.8 = f32[2,128,384]{2,1,0:T(8,128)} collective-permute-done((f32[2,128,384]{2,1,0:T(8,128)}, f32[2,128,384]{2,1,0:T(8,128)}, u32[]{:S(2)}, u32[]{:S(2)}) %collective-permute-start.8) | collective-permute-done | bytes 393248 | tf_op jit(solution)/shard_map/ppermute | solution.py:17
  (106 shorter events, 51.7 us)
Async XLA Ops:
  7.2 61.8 %copy-start = (bf16[384,3072]{1,0:T(8,128)(2,1)S(1)}, bf16[384,3072]{1,0:T(8,128)(2,1)}, u32[]{:S(2)}) copy-start(bf16[384,3072]{1,0:T(8,128)(2,1)} %param.10) | copy-start | bytes 7077892
  7.2 25.7 %copy-start.15 = (s32[2,3]{1,0:T(2,128)S(1)}, s32[2,3]{1,0:T(2,128)}, u32[]{:S(2)}) copy-start(s32[2,3]{1,0:T(2,128)} %param.13) | copy-start | bytes 76
  7.2 28.2 %copy-start.13 = (bf16[256,384]{1,0:T(8,128)(2,1)S(1)}, bf16[256,384]{1,0:T(8,128)(2,1)}, u32[]{:S(2)}) copy-start(bf16[256,384]{1,0:T(8,128)(2,1)} %param.7) | copy-start | bytes 589828
  7.2 61.8 %all-gather.2.cloned.1.call-start = ((), (), s32[]{:S(2)}) async-start(), calls=%async_computation.1 | async-start | bytes 1769472 | tf_op jit(solution)/shard_map/all_gather | solution.py:63
  8.4 48.5 %collective-permute-start.5 = (bf16[2,128,384]{2,1,0:T(8,128)(2,1)S(1)}, bf16[2,128,384]{2,1,0:T(8,128)(2,1)S(1)}, u32[]{:S(2)}, u32[]{:S(2)}) collective-permute-start(bf16[2,128,384]{2,1,0:T(8,128)(2,1)S(1)} %pad_maximum_fusion), channel_id=1, source_target_pairs={{24,0},{32,8},{40,16},{48,24},{56,32},{64,40},{72,48},{80,56},{88,... | collective-permute-start | bytes 589832 | tf_op jit(solution)/shard_map/ppermute | solution.py:17
  18.0 38.8 %collective-permute-start.4 = (bf16[2,128,384]{2,1,0:T(8,128)(2,1)S(1)}, bf16[2,128,384]{2,1,0:T(8,128)(2,1)S(1)}, u32[]{:S(2)}, u32[]{:S(2)}) collective-permute-start(bf16[2,128,384]{2,1,0:T(8,128)(2,1)S(1)} %pad_maximum_fusion), channel_id=1, source_target_pairs={{16,0},{24,8},{32,16},{40,24},{48,32},{56,40},{64,48},{72,56},{80,... | collective-permute-start | bytes 589832 | tf_op jit(solution)/shard_map/ppermute | solution.py:17
  20.2 36.5 %collective-permute-start.3 = (bf16[2,128,384]{2,1,0:T(8,128)(2,1)S(1)}, bf16[2,128,384]{2,1,0:T(8,128)(2,1)S(1)}, u32[]{:S(2)}, u32[]{:S(2)}) collective-permute-start(bf16[2,128,384]{2,1,0:T(8,128)(2,1)S(1)} %pad_maximum_fusion), channel_id=1, source_target_pairs={{8,0},{16,8},{24,16},{32,24},{40,32},{48,40},{56,48},{64,56},{72,6... | collective-permute-start | bytes 589832 | tf_op jit(solution)/shard_map/ppermute | solution.py:17
  22.1 30.7 %collective-permute-start.1 = (bf16[2,128,384]{2,1,0:T(8,128)(2,1)S(1)}, bf16[2,128,384]{2,1,0:T(8,128)(2,1)}, u32[]{:S(2)}, u32[]{:S(2)}) collective-permute-start(bf16[2,128,384]{2,1,0:T(8,128)(2,1)S(1)} %pad_maximum_fusion), channel_id=1, source_target_pairs={{0,16},{8,24},{16,32},{24,40},{32,48},{40,56},{48,64},{56,72},{64,... | collective-permute-start | bytes 589832 | tf_op jit(solution)/shard_map/ppermute | solution.py:17
  26.4 23.3 %collective-permute-start = (bf16[2,128,384]{2,1,0:T(8,128)(2,1)S(1)}, bf16[2,128,384]{2,1,0:T(8,128)(2,1)}, u32[]{:S(2)}, u32[]{:S(2)}) collective-permute-start(bf16[2,128,384]{2,1,0:T(8,128)(2,1)S(1)} %pad_maximum_fusion), channel_id=1, source_target_pairs={{0,24},{8,32},{16,40},{24,48},{32,56},{40,64},{48,72},{56,80},{64,... | collective-permute-start | bytes 589832 | tf_op jit(solution)/shard_map/ppermute | solution.py:17
  30.5 172.6 %reduce-scatter.4.cloned.1.call-start = ((), (), s32[]{:S(2)}) async-start(), calls=%async_computation.2 | async-start | bytes 1769472
  32.2 24.5 %copy-start.10 = (bf16[128,384]{1,0:T(8,128)(2,1)S(1)}, bf16[128,384]{1,0:T(8,128)(2,1)}, u32[]{:S(2)}) copy-start(bf16[128,384]{1,0:T(8,128)(2,1)} %param.9) | copy-start | bytes 294916
  32.2 24.5 %copy-start.11 = (bf16[128,384]{1,0:T(8,128)(2,1)S(1)}, bf16[128,384]{1,0:T(8,128)(2,1)}, u32[]{:S(2)}) copy-start(bf16[128,384]{1,0:T(8,128)(2,1)} %param.8) | copy-start | bytes 294916
  49.7 6.9 %collective-permute-start.2 = (bf16[2,128,384]{2,1,0:T(8,128)(2,1)S(1)}, bf16[2,128,384]{2,1,0:T(8,128)(2,1)S(1)}, u32[]{:S(2)}, u32[]{:S(2)}) collective-permute-start(bf16[2,128,384]{2,1,0:T(8,128)(2,1)S(1)} %pad_maximum_fusion), channel_id=1, source_target_pairs={{0,8},{8,16},{16,24},{24,32},{32,40},{40,48},{48,56},{56,64},{64,7... | collective-permute-start | bytes 589832 | tf_op jit(solution)/shard_map/ppermute | solution.py:17
  63.5 3.9 %copy-start.7 = (bf16[2,128,3,128]{3,2,1,0:T(4,128)(2,1)S(1)}, bf16[2,128,3,128]{3,2,1,0:T(4,128)(2,1)}, u32[]{:S(2)}) copy-start(bf16[2,128,3,128]{3,2,1,0:T(4,128)(2,1)} %reshape.98) | copy-start | bytes 589828
  85.4 3.4 %copy-start.9 = (bf16[2,384,3,128]{3,2,1,0:T(4,128)(2,1)S(1)}, bf16[2,384,3,128]{3,2,1,0:T(4,128)(2,1)}, u32[]{:S(2)}) copy-start(bf16[2,384,3,128]{3,2,1,0:T(4,128)(2,1)} %reshape_squeeze.6) | copy-start | bytes 1769476
  85.4 3.4 %copy-start.19 = (f32[2,3,128,384]{2,3,1,0:T(8,128)S(1)}, f32[2,3,128,384]{2,3,1,0:T(8,128)}, u32[]{:S(2)}) copy-start(f32[2,3,128,384]{2,3,1,0:T(8,128)} %get-tuple-element.27) | copy-start | bytes 3538948
  109.5 24.1 %collective-permute-start.10 = (f32[2,128,384]{2,1,0:T(8,128)S(1)}, f32[2,128,384]{2,1,0:T(8,128)S(1)}, u32[]{:S(2)}, u32[]{:S(2)}) collective-permute-start(f32[2,128,384]{2,1,0:T(8,128)S(1)} %bitcast.125), channel_id=1, source_target_pairs={{0,16},{8,24},{16,32},{24,40},{32,48},{40,56},{48,64},{56,72},{64,... | collective-permute-start | bytes 1179656 | tf_op jit(solution)/shard_map/ppermute | solution.py:17
  114.3 23.1 %copy-start.3 = (bf16[2,384,3,128]{1,3,2,0:T(8,128)(2,1)S(1)}, bf16[2,384,3,128]{1,3,2,0:T(8,128)(2,1)}, u32[]{:S(2)}) copy-start(bf16[2,384,3,128]{1,3,2,0:T(8,128)(2,1)} %copy.65) | copy-start | bytes 1769476
  114.3 23.2 %copy-start.5 = (bf16[2,3,128,384]{2,3,1,0:T(8,128)(2,1)S(1)}, bf16[2,3,128,384]{2,3,1,0:T(8,128)(2,1)}, u32[]{:S(2)}) copy-start(bf16[2,3,128,384]{2,3,1,0:T(8,128)(2,1)} %copy-done.4) | copy-start | bytes 1769476
  116.6 36.9 %collective-permute-start.11 = (f32[2,128,384]{2,1,0:T(8,128)}, f32[2,128,384]{2,1,0:T(8,128)}, u32[]{:S(2)}, u32[]{:S(2)}) collective-permute-start(f32[2,128,384]{2,1,0:T(8,128)} %bitcast.117), channel_id=1, source_target_pairs={{0,24},{8,32},{16,40},{24,48},{32,56},{40,64},{48,72},{56,80},{64,... | collective-permute-start | bytes 1179656 | tf_op jit(solution)/shard_map/ppermute | solution.py:17
  121.6 43.3 %collective-permute-start.6 = (f32[2,128,384]{2,1,0:T(8,128)}, f32[2,128,384]{2,1,0:T(8,128)}, u32[]{:S(2)}, u32[]{:S(2)}) collective-permute-start(f32[2,128,384]{2,1,0:T(8,128)} %bitcast.116), channel_id=1, source_target_pairs={{24,0},{32,8},{40,16},{48,24},{56,32},{64,40},{72,48},{80,56},{88,... | collective-permute-start | bytes 1179656 | tf_op jit(solution)/shard_map/ppermute | solution.py:17
  125.8 58.5 %collective-permute-start.7 = (f32[2,128,384]{2,1,0:T(8,128)}, f32[2,128,384]{2,1,0:T(8,128)}, u32[]{:S(2)}, u32[]{:S(2)}) collective-permute-start(f32[2,128,384]{2,1,0:T(8,128)} %bitcast.115), channel_id=1, source_target_pairs={{16,0},{24,8},{32,16},{40,24},{48,32},{56,40},{64,48},{72,56},{80,... | collective-permute-start | bytes 1179656 | tf_op jit(solution)/shard_map/ppermute | solution.py:17
  129.9 70.7 %collective-permute-start.8 = (f32[2,128,384]{2,1,0:T(8,128)}, f32[2,128,384]{2,1,0:T(8,128)}, u32[]{:S(2)}, u32[]{:S(2)}) collective-permute-start(f32[2,128,384]{2,1,0:T(8,128)} %bitcast.114), channel_id=1, source_target_pairs={{8,0},{16,8},{24,16},{32,24},{40,32},{48,40},{56,48},{64,56},{72,6... | collective-permute-start | bytes 1179656 | tf_op jit(solution)/shard_map/ppermute | solution.py:17
  134.3 66.3 %collective-permute-start.9 = (f32[2,128,384]{2,1,0:T(8,128)}, f32[2,128,384]{2,1,0:T(8,128)}, u32[]{:S(2)}, u32[]{:S(2)}) collective-permute-start(f32[2,128,384]{2,1,0:T(8,128)} %bitcast.113), channel_id=1, source_target_pairs={{0,8},{8,16},{16,24},{24,32},{32,40},{40,48},{48,56},{56,64},{64,7... | collective-permute-start | bytes 1179656 | tf_op jit(solution)/shard_map/ppermute | solution.py:17
  (10 other events, 17.2 us)
Sparse Core Ops, SparseCore 0:
  30.6 30.3 all-gather.1
  82.7 37.6 reduce-scatter.3
where the time goes:
time: 213 us; the launch traced here: 212 us
  waiting for transfers between devices  80.1 us (38%)
  local copies, waits for them, and re-layouts  51.5 us (24%)
  starting transfers between devices  45.8 us (22%)
  matrix products  16.1 us (8%)
  between operations  14.4 us (7%)
  other arithmetic  3.79 us (2%)
    ppermute x12, waiting for transfers between devices, from_behind(): return lax.ppermute(shard, axis, pairs)  80 us
    ppermute x12, starting transfers between devices, from_behind(): return lax.ppermute(shard, axis, pairs)  45.7 us
    unnamed x57, local copies, waits for them, and re-layouts  15.4 us
    another operation x4, local copies, waits for them, and re-layouts, local(): jnp.stack([key_terms.reshape(video_tiles * BLOCKS, TILE, head_cols), valu...  11.4 us
  transfers between devices with their start and end apart: 14, of which 7 were waited for; matrix products, arithmetic and copies ran while one was open for 24% of the time, Pallas kernels for 0%

commit v1 on v0

v1 whole, which is shorter than its diff:
```python
import functools
import math

import jax
import jax.numpy as jnp
from jax import lax
from jax.experimental import pallas as pl
from jax.experimental.pallas import tpu as pltpu
from jax.sharding import PartitionSpec as P

HEAD_DIM = 128
TILE = 128
BLOCKS = 3
LIST = 4
REACH = 3
SPAN = 2 * REACH + 1

VMEM = pltpu.VMEM
SMEM = pltpu.SMEM


def nt(a, b):
    return lax.dot_general(a, b, (((1,), (1,)), ((), ())), preferred_element_type=jnp.float32)


def tn(a, b):
    return lax.dot_general(a, b, (((0,), (0,)), ((), ())), preferred_element_type=jnp.float32)


def nn(a, b):
    return lax.dot_general(a, b, (((1,), (0,)), ((), ())), preferred_element_type=jnp.float32)


def grad_attended_kernel(where_ref, mine_ref, theirs_ref, weight_ref, out_ref):
    rows, cols = out_ref.shape
    total = None
    for n, ref in enumerate((mine_ref, theirs_ref)):
        for b in range(4):
            low = pl.multiple_of(where_ref[n * 4 + b] * cols, 128)
            term = nt(ref[pl.ds(b * rows, rows), :], weight_ref[:, pl.ds(low, cols)])
            total = term if total is None else total + term
    out_ref[...] = total.astype(out_ref.dtype)


def out_proj_kernel(where_ref, attended_ref, weight_ref, send_ref, keep_ref):
    rows, cols = attended_ref.shape
    attended = attended_ref[...]
    for n, ref in enumerate((send_ref, keep_ref)):
        for b in range(4):
            low = pl.multiple_of(where_ref[n * 4 + b] * cols, 128)
            ref[pl.ds(b * rows, rows), :] = nn(attended, weight_ref[:, pl.ds(low, cols)]).astype(ref.dtype)


def attention_kernel(slab_ref, align_ref, mask_ref, query_ref, grad_ref, *refs):
    tile_refs = refs[:SPAN]
    attended_ref, query_grad_ref = refs[SPAN : SPAN + 2]
    term_refs = refs[SPAN + 2 : 2 * SPAN + 2]
    region, sums = refs[2 * SPAN + 2 :]
    cols = query_ref.shape[1]
    heads = cols // HEAD_DIM
    tiles = query_ref.shape[0] // TILE
    score_scale = 1.0 / math.sqrt(HEAD_DIM)
    slab = slab_ref[0]
    for n in range(SPAN):
        region[pl.ds(n * 2 * TILE, 2 * TILE), :] = tile_refs[n][...]
    sums[...] = jnp.zeros_like(sums)
    for i in range(tiles):
        key_lows, live = [], []
        for b in range(BLOCKS):
            slot = mask_ref[i, b]
            picked = align_ref[slab, jnp.clip(slot, 0, LIST - 1)]
            local = jnp.clip(picked - slab + REACH, 0, SPAN - 1)
            live.append(slot >= 0)
            key_lows.append(pl.multiple_of(jnp.where(slot >= 0, local, 0) * (2 * TILE), 2 * TILE))
        for h in range(heads):
            rows, hcols = pl.ds(i * TILE, TILE), pl.ds(h * HEAD_DIM, HEAD_DIM)
            query = query_ref[rows, hcols]
            grad = grad_ref[rows, hcols]
            keys = [region[pl.ds(low, TILE), hcols] for low in key_lows]
            values = [region[pl.ds(low + TILE, TILE), hcols] for low in key_lows]
            scores = [
                jnp.where(live[b], nt(query, keys[b]) * score_scale, -jnp.inf) for b in range(BLOCKS)
            ]
            top = jnp.max(jnp.maximum(jnp.maximum(scores[0], scores[1]), scores[2]), -1, keepdims=True)
            exps = [jnp.exp(s - top) for s in scores]
            norm = jnp.sum(exps[0] + exps[1] + exps[2], -1, keepdims=True)
            probs = [e / norm for e in exps]
            weights = [p.astype(jnp.bfloat16) for p in probs]
            attended = nn(weights[0], values[0]) + nn(weights[1], values[1]) + nn(weights[2], values[2])
            attended = attended.astype(jnp.bfloat16)
            attended_ref[rows, hcols] = attended
            delta = jnp.sum(grad.astype(jnp.float32) * attended.astype(jnp.float32), -1, keepdims=True)
            grad_scores = [
                (probs[b] * (nt(grad, values[b]) - delta)).astype(jnp.bfloat16) for b in range(BLOCKS)
            ]
            query_grad = (
                nn(grad_scores[0], keys[0]) + nn(grad_scores[1], keys[1]) + nn(grad_scores[2], keys[2])
            )
            query_grad_ref[rows, hcols] = (query_grad * score_scale).astype(query_grad_ref.dtype)
            for b in range(BLOCKS):
                at_key, at_value = pl.ds(key_lows[b], TILE), pl.ds(key_lows[b] + TILE, TILE)
                sums[at_key, hcols] += tn(grad_scores[b], query) * score_scale
                sums[at_value, hcols] += tn(weights[b], grad)
    for n in range(SPAN):
        term_refs[n][...] = sums[pl.ds(n * 2 * TILE, 2 * TILE), :].astype(term_refs[n].dtype)


def vm():
    return pl.BlockSpec(memory_space=VMEM)


def sm():
    return pl.BlockSpec(memory_space=SMEM)


def local(queries, keys, values, out_weight, out_grad, align_lists, block_masks):
    slabs = lax.axis_size("tm")
    groups = lax.axis_size("head")
    chips = groups // 2
    slab = lax.axis_index("tm")
    group = lax.axis_index("head")
    chip, core = group // 2, group % 2
    rows, cols = queries.shape
    bf16, f32 = jnp.bfloat16, jnp.float32

    def along(x, by):
        return lax.ppermute(x, "tm", [(t, (t + by) % slabs) for t in range(slabs)])

    def across(x, by0, by1):
        pairs = [
            (2 * c + k, 2 * ((c + (by1 if k else by0)) % chips) + k)
            for c in range(chips)
            for k in range(2)
        ]
        return lax.ppermute(x, "head", pairs)

    def swap(x):
        return lax.ppermute(x, "head", [(g, g ^ 1) for g in range(groups)])

    own = jnp.concatenate([keys, values], 0)
    right, left = [], []
    r = l = own
    gathered = [out_grad]
    for n in range(REACH):
        r = along(r, 1)
        right.append(r)
        if n == 0:
            a_block = across(out_grad, 1, -1)
        l = along(l, -1)
        left.append(l)
        if n == 0:
            b_block = across(out_grad, -1, 1)
        if n == 1:
            c_block = across(a_block, 1, -1)
    mine = jnp.concatenate([out_grad, a_block, b_block, c_block], 0)
    theirs = swap(mine)

    def block_of(k, step):
        return 2 * ((chip + step) % chips) + k

    def order(k):
        step = jnp.where(k == 0, -1, 1)
        return [block_of(k, 0), block_of(k, step), block_of(k, -step), block_of(k, 2)]

    gather_order = jnp.stack(order(core) + order(1 - core)).astype(jnp.int32)
    scatter_order = jnp.stack(
        [block_of(1 - core, s) for s in range(4)] + [block_of(core, s) for s in range(4)]
    ).astype(jnp.int32)
    slab_array = jnp.full((1,), slab, jnp.int32)

    grad_attended = pl.pallas_call(
        grad_attended_kernel,
        out_shape=jax.ShapeDtypeStruct((rows, cols), bf16),
        in_specs=[sm(), vm(), vm(), vm()],
        out_specs=vm(),
        cost_estimate=pl.CostEstimate(
            flops=2 * rows * cols * 8 * cols, bytes_accessed=8 * cols * (rows + cols) * 2, transcendentals=0
        ),
        name="grad_attended",
    )(gather_order, mine, theirs, out_weight)

    tile_shape = jax.ShapeDtypeStruct((2 * TILE, cols), bf16)
    outs = pl.pallas_call(
        attention_kernel,
        out_shape=[jax.ShapeDtypeStruct((rows, cols), bf16)] * 2
        + [tile_shape] * REACH
        + [jax.ShapeDtypeStruct((2 * TILE, cols), f32)]
        + [tile_shape] * REACH,
        in_specs=[sm(), sm(), sm()] + [vm()] * (2 + SPAN),
        out_specs=[vm()] * (2 + SPAN),
        scratch_shapes=[VMEM((SPAN * 2 * TILE, cols), bf16), VMEM((SPAN * 2 * TILE, cols), f32)],
        cost_estimate=pl.CostEstimate(
            flops=14 * rows * cols * BLOCKS * TILE, bytes_accessed=20 * rows * cols * 2, transcendentals=rows * 1152
        ),
        name="attention",
    )(
        slab_array, align_lists, block_masks, queries, grad_attended,
        right[2], right[1], right[0], own, left[0], left[1], left[2],
    )
    attended, query_grad = outs[:2]
    terms = outs[2:]

    send, keep = pl.pallas_call(
        out_proj_kernel,
        out_shape=[jax.ShapeDtypeStruct((4 * rows, cols), bf16)] * 2,
        in_specs=[sm(), vm(), vm()],
        out_specs=[vm(), vm()],
        cost_estimate=pl.CostEstimate(
            flops=2 * rows * cols * 8 * cols, bytes_accessed=8 * cols * (rows + cols) * 2, transcendentals=0
        ),
        name="out_proj",
    )(scatter_order, attended, out_weight)

    def add(x, y):
        return (x.astype(f32) + y.astype(f32)).astype(bf16)

    rightward, leftward = terms[2 * REACH], terms[0]
    arrived = None
    for n in range(REACH - 1, -1, -1):
        rightward = along(rightward, 1)
        leftward = along(leftward, -1)
        if n:
            rightward = add(rightward, terms[REACH + n])
            leftward = add(leftward, terms[REACH - n])
        if n == REACH - 1:
            pair_sums = add(keep, swap(send)).reshape(4, rows, cols)
            arrived = [across(pair_sums[s], s, s) for s in (1, 3, 2)]
    total = terms[REACH] + rightward.astype(f32) + leftward.astype(f32)
    key_grad = total[:TILE].astype(bf16)
    value_grad = total[TILE:].astype(bf16)
    mixed = pair_sums[0].astype(f32)
    for part in arrived:
        mixed = mixed + part.astype(f32)
    return (mixed.astype(bf16), query_grad, key_grad, value_grad)


def solution(mesh):
    return jax.shard_map(
        local,
        mesh=mesh,
        in_specs=(
            P("tm", "head"),
            P("tm", "head"),
            P("tm", "head"),
            P("head", None),
            P("tm", "head"),
            P(),
            P("tm", None),
        ),
        out_specs=(P("tm", "head"), P("tm", "head"), P("tm", "head"), P("tm", "head")),
        check_vma=False,
    )
```

time: 213 us -> 136 us (0.64)
  the two profiles are of different devices: /device:TPU:91 before, /device:TPU:6 now
where the time goes in v1:
time: 136 us
  starting transfers between devices  87.1 us (64%)
  waiting for transfers between devices  25.4 us (19%)
  Pallas kernels  15.3 us (11%)
  local copies, waits for them, and re-layouts  5.44 us (4%)
    ppermute x12, starting transfers between devices, along(): return lax.ppermute(x, 'tm', [(t, (t + by) % slabs) for t in range(slabs)])  58.9 us
    ppermute x6, starting transfers between devices, across(): return lax.ppermute(x, 'head', pairs)  24.2 us
    ppermute x12, waiting for transfers between devices, along(): return lax.ppermute(x, 'tm', [(t, (t + by) % slabs) for t in range(slabs)])  14.3 us
    ppermute x6, waiting for transfers between devices, across(): return lax.ppermute(x, 'head', pairs)  11 us
    pallas_call x1, Pallas kernels, local(): pl.pallas_call(attention_kernel, out_shape=[jax.ShapeDtypeStruct((rows, c...  7.39 us
    pallas_call x1, Pallas kernels, local(): pl.pallas_call(grad_attended_kernel, out_shape=jax.ShapeDtypeStruct((rows...  3.99 us
    ppermute x2, starting transfers between devices, swap(): return lax.ppermute(x, 'head', [(g, g ^ 1) for g in range(groups)])  3.96 us
    pallas_call x1, Pallas kernels, local(): pl.pallas_call(out_proj_kernel, out_shape=[jax.ShapeDtypeStruct((4 * rows...  3.88 us
  transfers between devices with their start and end apart: 20, of which 12 were waited for; matrix products, arithmetic and copies ran while one was open for 3% of the time, Pallas kernels for 6%

profile of v1, /device:TPU:6, one launch (start us, length us, event | category | flops | bytes accessed | tf_op | source)
XLA Modules:
  0.0 135.7 jit_solution(4052616576932869309)
XLA Ops:
  0.7 7.9 %collective-permute-start = (bf16[256,384]{1,0:T(8,128)(2,1)}, bf16[256,384]{1,0:T(8,128)(2,1)S(1)}, u32[]{:S(2)}, u32[]{:S(2)}) collective-permute-start(bf16[256,384]{1,0:T(8,128)(2,1)} %param.11), channel_id=1, source_target_pairs={{0,2},{1,7},{2,4},{3,1},{4,6},{5,3},{6,0},{7,5},{8,10},{9,15},{10,... | collective-permute-start | bytes 589832 | tf_op jit(solution)/shard_map/ppermute | solution.py:135
  12.0 5.5 %collective-permute-start.2 = (bf16[256,384]{1,0:T(8,128)(2,1)S(1)}, bf16[256,384]{1,0:T(8,128)(2,1)S(1)}, u32[]{:S(2)}, u32[]{:S(2)}) collective-permute-start(bf16[256,384]{1,0:T(8,128)(2,1)S(1)} %collective-permute-done), channel_id=1, source_target_pairs={{0,2},{1,7},{2,4},{3,1},{4,6},{5,3},{6,0},{7,5},{8,10},{9,15},{10,... | collective-permute-start | bytes 589832 | tf_op jit(solution)/shard_map/ppermute | solution.py:135
  18.4 2.3 %collective-permute-done.2 = bf16[256,384]{1,0:T(8,128)(2,1)S(1)} collective-permute-done((bf16[256,384]{1,0:T(8,128)(2,1)S(1)}, bf16[256,384]{1,0:T(8,128)(2,1)S(1)}, u32[]{:S(2)}, u32[]{:S(2)}) %collective-permute-start.2) | collective-permute-done | bytes 196640 | tf_op jit(solution)/shard_map/ppermute | solution.py:135
  22.7 10.1 %collective-permute-start.7 = (bf16[256,384]{1,0:T(8,128)(2,1)S(1)}, bf16[256,384]{1,0:T(8,128)(2,1)S(1)}, u32[]{:S(2)}, u32[]{:S(2)}) collective-permute-start(bf16[256,384]{1,0:T(8,128)(2,1)S(1)} %constant_dynamic-update-slice_fusion.4.refs_3_), channel_id=1, source_target_pairs={{0,504},{8,0},{16,8},{24,16},{32,24},{40,32},{48,40},{56,48},{64,5... | collective-permute-start | bytes 589832 | tf_op jit(solution)/shard_map/ppermute | solution.py:127
  34.7 2.9 %collective-permute-done.7.refs_4_ = bf16[256,384]{1,0:T(8,128)(2,1)S(1)} collective-permute-done((bf16[256,384]{1,0:T(8,128)(2,1)S(1)}, bf16[256,384]{1,0:T(8,128)(2,1)S(1)}, u32[]{:S(2)}, u32[]{:S(2)}) %collective-permute-start.7) | collective-permute-done | bytes 196640 | tf_op jit(solution)/shard_map/ppermute | solution.py:127
  37.6 7.7 %collective-permute-start.8 = (bf16[256,384]{1,0:T(8,128)(2,1)S(1)}, bf16[256,384]{1,0:T(8,128)(2,1)S(1)}, u32[]{:S(2)}, u32[]{:S(2)}) collective-permute-start(bf16[256,384]{1,0:T(8,128)(2,1)S(1)} %collective-permute-done.7.refs_4_), channel_id=1, source_target_pairs={{0,504},{8,0},{16,8},{24,16},{32,24},{40,32},{48,40},{56,48},{64,5... | collective-permute-start | bytes 589832 | tf_op jit(solution)/shard_map/ppermute | solution.py:127
  47.3 2.0 %collective-permute-done.8.refs_5_ = bf16[256,384]{1,0:T(8,128)(2,1)S(1)} collective-permute-done((bf16[256,384]{1,0:T(8,128)(2,1)S(1)}, bf16[256,384]{1,0:T(8,128)(2,1)S(1)}, u32[]{:S(2)}, u32[]{:S(2)}) %collective-permute-start.8) | collective-permute-done | bytes 196640 | tf_op jit(solution)/shard_map/ppermute | solution.py:127
  49.3 7.7 %collective-permute-start.9 = (bf16[256,384]{1,0:T(8,128)(2,1)S(1)}, bf16[256,384]{1,0:T(8,128)(2,1)S(1)}, u32[]{:S(2)}, u32[]{:S(2)}) collective-permute-start(bf16[256,384]{1,0:T(8,128)(2,1)S(1)} %collective-permute-done.8.refs_5_), channel_id=1, source_target_pairs={{0,504},{8,0},{16,8},{24,16},{32,24},{40,32},{48,40},{56,48},{64,5... | collective-permute-start | bytes 589832 | tf_op jit(solution)/shard_map/ppermute | solution.py:127
  61.3 4.0 %grad_attended.1.grad_ref = bf16[256,384]{1,0:T(8,128)(2,1)} custom-call(s32[8]{0:T(128)} %stack.59.where_ref, bf16[1024,384]{1,0:T(8,128)(2,1)} %copy-done, bf16[1024,384]{1,0:T(8,128)(2,1)} %copy-done.1, bf16[384,3072]{1,0:T(8,128)(2,1)} %weight_ref.3), custom_call_target="tpu_custom_call" | custom-call | flops 603979776 | bytes 3932160 | tf_op jit(solution)/shard_map/grad_attended/pallas_call | solution.py:171
  65.3 2.5 %collective-permute-done.6.refs_0_ = bf16[256,384]{1,0:T(8,128)(2,1)S(1)} collective-permute-done((bf16[256,384]{1,0:T(8,128)(2,1)S(1)}, bf16[256,384]{1,0:T(8,128)(2,1)S(1)}, u32[]{:S(2)}, u32[]{:S(2)}) %collective-permute-start.6) | collective-permute-done | bytes 196640 | tf_op jit(solution)/shard_map/ppermute | solution.py:127
  68.5 7.4 %attention.1 = (bf16[256,384]{1,0:T(8,128)(2,1)}, bf16[256,384]{1,0:T(8,128)(2,1)}, bf16[256,384]{1,0:T(8,128)(2,1)}, bf16[256,384]{1,0:T(8,128)(2,1)}, bf16[256...) custom-call(s32[1]{0:T(128)} %bitcast.8.slab_ref, ...), custom_call_target="tpu_custom_call" | custom-call | flops 528482304 | bytes 3932160 | tf_op jit(solution)/shard_map/attention/pallas_call | solution.py:183
  75.9 2.0 %collective-permute-start.14 = (bf16[256,384]{1,0:T(8,128)(2,1)}, bf16[256,384]{1,0:T(8,128)(2,1)S(1)}, u32[]{:S(2)}, u32[]{:S(2)}) collective-permute-start(bf16[256,384]{1,0:T(8,128)(2,1)} %get-tuple-element.20), channel_id=1, source_target_pairs={{0,8},{8,16},{16,24},{24,32},{32,40},{40,48},{48,56},{56,64},{64,7... | collective-permute-start | bytes 589832 | tf_op jit(solution)/shard_map/ppermute | solution.py:127
  78.7 7.2 %collective-permute-start.17 = (bf16[256,384]{1,0:T(8,128)(2,1)}, bf16[256,384]{1,0:T(8,128)(2,1)S(1)}, u32[]{:S(2)}, u32[]{:S(2)}) collective-permute-start(bf16[256,384]{1,0:T(8,128)(2,1)} %get-tuple-element.23), channel_id=1, source_target_pairs={{0,504},{8,0},{16,8},{24,16},{32,24},{40,32},{48,40},{56,48},{64,5... | collective-permute-start | bytes 589832 | tf_op jit(solution)/shard_map/ppermute | solution.py:127
  85.9 3.9 %out_proj.1 = (bf16[1024,384]{1,0:T(8,128)(2,1)}, bf16[1024,384]{1,0:T(8,128)(2,1)}) custom-call(s32[8]{0:T(128)} %stack.54.where_ref, bf16[256,384]{1,0:T(8,128)(2,1)} %get-tuple-element.15.attended_ref, bf16[384,3072]{1,0:T(8,128)(2,1)} %weight_ref.3), custom_call_target="tpu_custom_call" | custom-call | flops 603979776 | bytes 3932160 | tf_op jit(solution)/shard_map/out_proj/pallas_call | solution.py:203
  89.8 2.0 %collective-permute-start.10 = (bf16[1024,384]{1,0:T(8,128)(2,1)}, bf16[1024,384]{1,0:T(8,128)(2,1)S(1)}, u32[]{:S(2)}, u32[]{:S(2)}) collective-permute-start(bf16[1024,384]{1,0:T(8,128)(2,1)} %get-tuple-element.17), channel_id=1, source_target_pairs={{0,1},{1,0},{2,3},{3,2},{4,5},{5,4},{6,7},{7,6},{8,9},{9,8},{10,11... | collective-permute-start | bytes 2359304 | tf_op jit(solution)/shard_map/ppermute | solution.py:138
  91.9 2.1 %collective-permute-start.15 = (bf16[256,384]{1,0:T(8,128)(2,1)S(1)}, bf16[256,384]{1,0:T(8,128)(2,1)S(1)}, u32[]{:S(2)}, u32[]{:S(2)}) collective-permute-start(bf16[256,384]{1,0:T(8,128)(2,1)S(1)} %add_convert_fusion.5), channel_id=1, source_target_pairs={{0,8},{8,16},{16,24},{24,32},{32,40},{40,48},{48,56},{56,64},{64,7... | collective-permute-start | bytes 589832 | tf_op jit(solution)/shard_map/ppermute | solution.py:127
  94.1 7.2 %collective-permute-start.18 = (bf16[256,384]{1,0:T(8,128)(2,1)S(1)}, bf16[256,384]{1,0:T(8,128)(2,1)S(1)}, u32[]{:S(2)}, u32[]{:S(2)}) collective-permute-start(bf16[256,384]{1,0:T(8,128)(2,1)S(1)} %add_convert_fusion.3), channel_id=1, source_target_pairs={{0,504},{8,0},{16,8},{24,16},{32,24},{40,32},{48,40},{56,48},{64,5... | collective-permute-start | bytes 589832 | tf_op jit(solution)/shard_map/ppermute | solution.py:127
  101.3 3.3 %collective-permute-done.15 = bf16[256,384]{1,0:T(8,128)(2,1)S(1)} collective-permute-done((bf16[256,384]{1,0:T(8,128)(2,1)S(1)}, bf16[256,384]{1,0:T(8,128)(2,1)S(1)}, u32[]{:S(2)}, u32[]{:S(2)}) %collective-permute-start.15) | collective-permute-done | bytes 196640 | tf_op jit(solution)/shard_map/ppermute | solution.py:127
  106.7 7.2 %collective-permute-start.19 = (bf16[256,384]{1,0:T(8,128)(2,1)S(1)}, bf16[256,384]{1,0:T(8,128)(2,1)S(1)}, u32[]{:S(2)}, u32[]{:S(2)}) collective-permute-start(bf16[256,384]{1,0:T(8,128)(2,1)S(1)} %add_convert_fusion.2), channel_id=1, source_target_pairs={{0,504},{8,0},{16,8},{24,16},{32,24},{40,32},{48,40},{56,48},{64,5... | collective-permute-start | bytes 589832 | tf_op jit(solution)/shard_map/ppermute | solution.py:127
  113.9 2.4 %collective-permute-done.16 = bf16[256,384]{1,0:T(8,128)(2,1)S(1)} collective-permute-done((bf16[256,384]{1,0:T(8,128)(2,1)S(1)}, bf16[256,384]{1,0:T(8,128)(2,1)S(1)}, u32[]{:S(2)}, u32[]{:S(2)}) %collective-permute-start.16) | collective-permute-done | bytes 196640 | tf_op jit(solution)/shard_map/ppermute | solution.py:127
  117.9 4.0 %collective-permute-start.11 = (bf16[256,384]{1,0:T(8,128)(2,1)S(1)}, bf16[256,384]{1,0:T(8,128)(2,1)S(1)}, u32[]{:S(2)}, u32[]{:S(2)}) collective-permute-start(bf16[256,384]{1,0:T(8,128)(2,1)S(1)} %get-tuple-element.26), channel_id=1, source_target_pairs={{0,2},{1,3},{2,4},{3,5},{4,6},{5,7},{6,0},{7,1},{8,10},{9,11},{10,... | collective-permute-start | bytes 589832 | tf_op jit(solution)/shard_map/ppermute | solution.py:135
  122.0 3.0 %collective-permute-start.13 = (bf16[256,384]{1,0:T(8,128)(2,1)S(1)}, bf16[256,384]{1,0:T(8,128)(2,1)S(1)}, u32[]{:S(2)}, u32[]{:S(2)}) collective-permute-start(bf16[256,384]{1,0:T(8,128)(2,1)S(1)} %get-tuple-element.27), channel_id=1, source_target_pairs={{0,4},{1,5},{2,6},{3,7},{4,0},{5,1},{6,2},{7,3},{8,12},{9,13},{10,... | collective-permute-start | bytes 589832 | tf_op jit(solution)/shard_map/ppermute | solution.py:135
  129.3 3.4 %collective-permute-done.13 = bf16[256,384]{1,0:T(8,128)(2,1)S(1)} collective-permute-done((bf16[256,384]{1,0:T(8,128)(2,1)S(1)}, bf16[256,384]{1,0:T(8,128)(2,1)S(1)}, u32[]{:S(2)}, u32[]{:S(2)}) %collective-permute-start.13) | collective-permute-done | bytes 196640 | tf_op jit(solution)/shard_map/ppermute | solution.py:135
  132.7 2.3 %collective-permute-done.12 = bf16[256,384]{1,0:T(8,128)(2,1)S(1)} collective-permute-done((bf16[256,384]{1,0:T(8,128)(2,1)S(1)}, bf16[256,384]{1,0:T(8,128)(2,1)S(1)}, u32[]{:S(2)}, u32[]{:S(2)}) %collective-permute-start.12) | collective-permute-done | bytes 196640 | tf_op jit(solution)/shard_map/ppermute | solution.py:135
  (73 shorter events, 24.5 us)
Async XLA Ops:
  0.7 58.4 %copy-start.11 = (s32[64,4]{0,1:T(4,128)S(1)}, s32[64,4]{0,1:T(4,128)}, u32[]{:S(2)}) copy-start(s32[64,4]{0,1:T(4,128)} %param.12) | copy-start | bytes 3076
  0.7 11.4 %collective-permute-start = (bf16[256,384]{1,0:T(8,128)(2,1)}, bf16[256,384]{1,0:T(8,128)(2,1)S(1)}, u32[]{:S(2)}, u32[]{:S(2)}) collective-permute-start(bf16[256,384]{1,0:T(8,128)(2,1)} %param.11), channel_id=1, source_target_pairs={{0,2},{1,7},{2,4},{3,1},{4,6},{5,3},{6,0},{7,5},{8,10},{9,15},{10,... | collective-permute-start | bytes 589832 | tf_op jit(solution)/shard_map/ppermute | solution.py:135
  8.5 9.8 %collective-permute-start.1 = (bf16[256,384]{1,0:T(8,128)(2,1)}, bf16[256,384]{1,0:T(8,128)(2,1)S(1)}, u32[]{:S(2)}, u32[]{:S(2)}) collective-permute-start(bf16[256,384]{1,0:T(8,128)(2,1)} %param.11), channel_id=1, source_target_pairs={{0,6},{1,3},{2,0},{3,5},{4,2},{5,7},{6,4},{7,1},{8,14},{9,11},{10,... | collective-permute-start | bytes 589832 | tf_op jit(solution)/shard_map/ppermute | solution.py:135
  12.0 8.7 %collective-permute-start.2 = (bf16[256,384]{1,0:T(8,128)(2,1)S(1)}, bf16[256,384]{1,0:T(8,128)(2,1)S(1)}, u32[]{:S(2)}, u32[]{:S(2)}) collective-permute-start(bf16[256,384]{1,0:T(8,128)(2,1)S(1)} %collective-permute-done), channel_id=1, source_target_pairs={{0,2},{1,7},{2,4},{3,1},{4,6},{5,3},{6,0},{7,5},{8,10},{9,15},{10,... | collective-permute-start | bytes 589832 | tf_op jit(solution)/shard_map/ppermute | solution.py:135
  20.7 39.7 %copy-start = (bf16[1024,384]{1,0:T(8,128)(2,1)}, bf16[1024,384]{1,0:T(8,128)(2,1)S(1)}, u32[]{:S(2)}) copy-start(bf16[1024,384]{1,0:T(8,128)(2,1)S(1)} %constant_dynamic-update-slice_fusion.mine_ref) | copy-start | bytes 2359300
  20.7 39.7 %collective-permute-start.3 = (bf16[1024,384]{1,0:T(8,128)(2,1)S(1)}, bf16[1024,384]{1,0:T(8,128)(2,1)S(1)}, u32[]{:S(2)}, u32[]{:S(2)}) collective-permute-start(bf16[1024,384]{1,0:T(8,128)(2,1)S(1)} %constant_dynamic-update-slice_fusion.mine_ref), channel_id=1, source_target_pairs={{0,1},{1,0},{2,3},{3,2},{4,5},{5,4},{6,7},{7,6},{8,9},{9,8},{10,11... | collective-permute-start | bytes 2359304 | tf_op jit(solution)/shard_map/ppermute | solution.py:138
  22.7 42.6 %copy-start.10 = (bf16[256,384]{1,0:T(8,128)(2,1)}, bf16[256,384]{1,0:T(8,128)(2,1)S(1)}, u32[]{:S(2)}) copy-start(bf16[256,384]{1,0:T(8,128)(2,1)S(1)} %constant_dynamic-update-slice_fusion.4.refs_3_) | copy-start | bytes 589828
  22.7 14.9 %collective-permute-start.7 = (bf16[256,384]{1,0:T(8,128)(2,1)S(1)}, bf16[256,384]{1,0:T(8,128)(2,1)S(1)}, u32[]{:S(2)}, u32[]{:S(2)}) collective-permute-start(bf16[256,384]{1,0:T(8,128)(2,1)S(1)} %constant_dynamic-update-slice_fusion.4.refs_3_), channel_id=1, source_target_pairs={{0,504},{8,0},{16,8},{24,16},{32,24},{40,32},{48,40},{56,48},{64,5... | collective-permute-start | bytes 589832 | tf_op jit(solution)/shard_map/ppermute | solution.py:127
  32.8 12.5 %collective-permute-start.4 = (bf16[256,384]{1,0:T(8,128)(2,1)S(1)}, bf16[256,384]{1,0:T(8,128)(2,1)S(1)}, u32[]{:S(2)}, u32[]{:S(2)}) collective-permute-start(bf16[256,384]{1,0:T(8,128)(2,1)S(1)} %constant_dynamic-update-slice_fusion.4.refs_3_), channel_id=1, source_target_pairs={{0,8},{8,16},{16,24},{24,32},{32,40},{40,48},{48,56},{56,64},{64,7... | collective-permute-start | bytes 589832 | tf_op jit(solution)/shard_map/ppermute | solution.py:127
  37.6 30.3 %copy-start.12 = (bf16[256,384]{1,0:T(8,128)(2,1)}, bf16[256,384]{1,0:T(8,128)(2,1)S(1)}, u32[]{:S(2)}) copy-start(bf16[256,384]{1,0:T(8,128)(2,1)S(1)} %collective-permute-done.7.refs_4_) | copy-start | bytes 589828
  37.6 11.6 %collective-permute-start.8 = (bf16[256,384]{1,0:T(8,128)(2,1)S(1)}, bf16[256,384]{1,0:T(8,128)(2,1)S(1)}, u32[]{:S(2)}, u32[]{:S(2)}) collective-permute-start(bf16[256,384]{1,0:T(8,128)(2,1)S(1)} %collective-permute-done.7.refs_4_), channel_id=1, source_target_pairs={{0,504},{8,0},{16,8},{24,16},{32,24},{40,32},{48,40},{56,48},{64,5... | collective-permute-start | bytes 589832 | tf_op jit(solution)/shard_map/ppermute | solution.py:127
  45.3 11.6 %collective-permute-start.5 = (bf16[256,384]{1,0:T(8,128)(2,1)S(1)}, bf16[256,384]{1,0:T(8,128)(2,1)S(1)}, u32[]{:S(2)}, u32[]{:S(2)}) collective-permute-start(bf16[256,384]{1,0:T(8,128)(2,1)S(1)} %collective-permute-done.4.refs_2_), channel_id=1, source_target_pairs={{0,8},{8,16},{16,24},{24,32},{32,40},{40,48},{48,56},{56,64},{64,7... | collective-permute-start | bytes 589832 | tf_op jit(solution)/shard_map/ppermute | solution.py:127
  49.3 16.1 %collective-permute-start.9 = (bf16[256,384]{1,0:T(8,128)(2,1)S(1)}, bf16[256,384]{1,0:T(8,128)(2,1)S(1)}, u32[]{:S(2)}, u32[]{:S(2)}) collective-permute-start(bf16[256,384]{1,0:T(8,128)(2,1)S(1)} %collective-permute-done.8.refs_5_), channel_id=1, source_target_pairs={{0,504},{8,0},{16,8},{24,16},{32,24},{40,32},{48,40},{56,48},{64,5... | collective-permute-start | bytes 589832 | tf_op jit(solution)/shard_map/ppermute | solution.py:127
  57.0 10.9 %collective-permute-start.6 = (bf16[256,384]{1,0:T(8,128)(2,1)S(1)}, bf16[256,384]{1,0:T(8,128)(2,1)S(1)}, u32[]{:S(2)}, u32[]{:S(2)}) collective-permute-start(bf16[256,384]{1,0:T(8,128)(2,1)S(1)} %collective-permute-done.5.refs_1_), channel_id=1, source_target_pairs={{0,8},{8,16},{16,24},{24,32},{32,40},{40,48},{48,56},{56,64},{64,7... | collective-permute-start | bytes 589832 | tf_op jit(solution)/shard_map/ppermute | solution.py:127
  75.9 15.9 %collective-permute-start.14 = (bf16[256,384]{1,0:T(8,128)(2,1)}, bf16[256,384]{1,0:T(8,128)(2,1)S(1)}, u32[]{:S(2)}, u32[]{:S(2)}) collective-permute-start(bf16[256,384]{1,0:T(8,128)(2,1)} %get-tuple-element.20), channel_id=1, source_target_pairs={{0,8},{8,16},{16,24},{24,32},{32,40},{40,48},{48,56},{56,64},{64,7... | collective-permute-start | bytes 589832 | tf_op jit(solution)/shard_map/ppermute | solution.py:127
  78.7 15.3 %collective-permute-start.17 = (bf16[256,384]{1,0:T(8,128)(2,1)}, bf16[256,384]{1,0:T(8,128)(2,1)S(1)}, u32[]{:S(2)}, u32[]{:S(2)}) collective-permute-start(bf16[256,384]{1,0:T(8,128)(2,1)} %get-tuple-element.23), channel_id=1, source_target_pairs={{0,504},{8,0},{16,8},{24,16},{32,24},{40,32},{48,40},{56,48},{64,5... | collective-permute-start | bytes 589832 | tf_op jit(solution)/shard_map/ppermute | solution.py:127
  89.8 27.9 %collective-permute-start.10 = (bf16[1024,384]{1,0:T(8,128)(2,1)}, bf16[1024,384]{1,0:T(8,128)(2,1)S(1)}, u32[]{:S(2)}, u32[]{:S(2)}) collective-permute-start(bf16[1024,384]{1,0:T(8,128)(2,1)} %get-tuple-element.17), channel_id=1, source_target_pairs={{0,1},{1,0},{2,3},{3,2},{4,5},{5,4},{6,7},{7,6},{8,9},{9,8},{10,11... | collective-permute-start | bytes 2359304 | tf_op jit(solution)/shard_map/ppermute | solution.py:138
  91.9 12.7 %collective-permute-start.15 = (bf16[256,384]{1,0:T(8,128)(2,1)S(1)}, bf16[256,384]{1,0:T(8,128)(2,1)S(1)}, u32[]{:S(2)}, u32[]{:S(2)}) collective-permute-start(bf16[256,384]{1,0:T(8,128)(2,1)S(1)} %add_convert_fusion.5), channel_id=1, source_target_pairs={{0,8},{8,16},{16,24},{24,32},{32,40},{40,48},{48,56},{56,64},{64,7... | collective-permute-start | bytes 589832 | tf_op jit(solution)/shard_map/ppermute | solution.py:127
  94.1 12.5 %collective-permute-start.18 = (bf16[256,384]{1,0:T(8,128)(2,1)S(1)}, bf16[256,384]{1,0:T(8,128)(2,1)S(1)}, u32[]{:S(2)}, u32[]{:S(2)}) collective-permute-start(bf16[256,384]{1,0:T(8,128)(2,1)S(1)} %add_convert_fusion.3), channel_id=1, source_target_pairs={{0,504},{8,0},{16,8},{24,16},{32,24},{40,32},{48,40},{56,48},{64,5... | collective-permute-start | bytes 589832 | tf_op jit(solution)/shard_map/ppermute | solution.py:127
  104.6 11.7 %collective-permute-start.16 = (bf16[256,384]{1,0:T(8,128)(2,1)S(1)}, bf16[256,384]{1,0:T(8,128)(2,1)S(1)}, u32[]{:S(2)}, u32[]{:S(2)}) collective-permute-start(bf16[256,384]{1,0:T(8,128)(2,1)S(1)} %add_convert_fusion.4), channel_id=1, source_target_pairs={{0,8},{8,16},{16,24},{24,32},{32,40},{40,48},{48,56},{56,64},{64,7... | collective-permute-start | bytes 589832 | tf_op jit(solution)/shard_map/ppermute | solution.py:127
  106.7 10.9 %collective-permute-start.19 = (bf16[256,384]{1,0:T(8,128)(2,1)S(1)}, bf16[256,384]{1,0:T(8,128)(2,1)S(1)}, u32[]{:S(2)}, u32[]{:S(2)}) collective-permute-start(bf16[256,384]{1,0:T(8,128)(2,1)S(1)} %add_convert_fusion.2), channel_id=1, source_target_pairs={{0,504},{8,0},{16,8},{24,16},{32,24},{40,32},{48,40},{56,48},{64,5... | collective-permute-start | bytes 589832 | tf_op jit(solution)/shard_map/ppermute | solution.py:127
  117.9 11.3 %collective-permute-start.11 = (bf16[256,384]{1,0:T(8,128)(2,1)S(1)}, bf16[256,384]{1,0:T(8,128)(2,1)S(1)}, u32[]{:S(2)}, u32[]{:S(2)}) collective-permute-start(bf16[256,384]{1,0:T(8,128)(2,1)S(1)} %get-tuple-element.26), channel_id=1, source_target_pairs={{0,2},{1,3},{2,4},{3,5},{4,6},{5,7},{6,0},{7,1},{8,10},{9,11},{10,... | collective-permute-start | bytes 589832 | tf_op jit(solution)/shard_map/ppermute | solution.py:135
  122.0 10.7 %collective-permute-start.13 = (bf16[256,384]{1,0:T(8,128)(2,1)S(1)}, bf16[256,384]{1,0:T(8,128)(2,1)S(1)}, u32[]{:S(2)}, u32[]{:S(2)}) collective-permute-start(bf16[256,384]{1,0:T(8,128)(2,1)S(1)} %get-tuple-element.27), channel_id=1, source_target_pairs={{0,4},{1,5},{2,6},{3,7},{4,0},{5,1},{6,2},{7,3},{8,12},{9,13},{10,... | collective-permute-start | bytes 589832 | tf_op jit(solution)/shard_map/ppermute | solution.py:135
  125.0 10.0 %collective-permute-start.12 = (bf16[256,384]{1,0:T(8,128)(2,1)S(1)}, bf16[256,384]{1,0:T(8,128)(2,1)S(1)}, u32[]{:S(2)}, u32[]{:S(2)}) collective-permute-start(bf16[256,384]{1,0:T(8,128)(2,1)S(1)} %get-tuple-element.28), channel_id=1, source_target_pairs={{0,6},{1,7},{2,0},{3,1},{4,2},{5,3},{6,4},{7,5},{8,14},{9,15},{10,... | collective-permute-start | bytes 589832 | tf_op jit(solution)/shard_map/ppermute | solution.py:135
  (14 other events, 217.3 us)

commit v2 on v1

v2 whole, which is shorter than its diff:
```python
import functools
import math

import jax
import jax.numpy as jnp
from jax import lax
from jax.experimental import pallas as pl
from jax.experimental.pallas import tpu as pltpu
from jax.sharding import PartitionSpec as P


HEAD_DIM = 128
TILE = 128
BLOCKS = 3
LIST = 4
REACH = 3
SPAN = 2 * REACH + 1
LIMIT = 24 * 1024 * 1024

VMEM = pltpu.VMEM
SMEM = pltpu.SMEM


def nt(a, b):
    return lax.dot_general(a, b, (((1,), (1,)), ((), ())), preferred_element_type=jnp.float32)


def tn(a, b):
    return lax.dot_general(a, b, (((0,), (0,)), ((), ())), preferred_element_type=jnp.float32)


def nn(a, b):
    return lax.dot_general(a, b, (((1,), (0,)), ((), ())), preferred_element_type=jnp.float32)


def block_of(group, flip, step, chips):
    return (((group >> 1) + step) & (chips - 1)) * 2 + ((group & 1) ^ flip)


def grad_attended_kernel(chips, group_ref, mine_ref, theirs_ref, weight_ref, out_ref):
    rows, cols = out_ref.shape
    group = group_ref[0]
    total = None
    for flip, ref in enumerate((mine_ref, theirs_ref)):
        step = (((group & 1) ^ flip) << 1) - 1
        for b, by in enumerate((0, step, -step, 2)):
            low = pl.multiple_of(block_of(group, flip, by, chips) * cols, 128)
            term = nt(ref[pl.ds(b * rows, rows), :], weight_ref[:, pl.ds(low, cols)])
            total = term if total is None else total + term
    out_ref[...] = total.astype(out_ref.dtype)


def out_proj_kernel(chips, group_ref, attended_ref, weight_ref, send_ref, keep_ref):
    rows, cols = attended_ref.shape
    group = group_ref[0]
    attended = attended_ref[...]
    for flip, ref in ((1, send_ref), (0, keep_ref)):
        for b in range(4):
            low = pl.multiple_of(block_of(group, flip, b, chips) * cols, 128)
            ref[pl.ds(b * rows, rows), :] = nn(attended, weight_ref[:, pl.ds(low, cols)]).astype(ref.dtype)


def attention_kernel(slab_ref, align_ref, mask_ref, query_ref, grad_ref, *refs):
    tile_refs = refs[:SPAN]
    attended_ref, query_grad_ref = refs[SPAN : SPAN + 2]
    term_refs = refs[SPAN + 2 : 2 * SPAN + 2]
    region, sums = refs[2 * SPAN + 2 :]
    cols = query_ref.shape[1]
    heads = cols // HEAD_DIM
    tiles = query_ref.shape[0] // TILE
    score_scale = 1.0 / math.sqrt(HEAD_DIM)
    slab = slab_ref[0]
    for n in range(SPAN):
        region[pl.ds(n * 2 * TILE, 2 * TILE), :] = tile_refs[n][...]
    sums[...] = jnp.zeros_like(sums)
    for i in range(tiles):
        key_lows, live = [], []
        for b in range(BLOCKS):
            slot = mask_ref[i, b]
            picked = align_ref[jnp.clip(slot, 0, LIST - 1), slab]
            local = jnp.clip(picked - slab + REACH, 0, SPAN - 1)
            live.append(slot >= 0)
            key_lows.append(pl.multiple_of(jnp.where(slot >= 0, local, 0) * (2 * TILE), 2 * TILE))
        for h in range(heads):
            rows, hcols = pl.ds(i * TILE, TILE), pl.ds(h * HEAD_DIM, HEAD_DIM)
            query = query_ref[rows, hcols]
            grad = grad_ref[rows, hcols]
            keys = [region[pl.ds(low, TILE), hcols] for low in key_lows]
            values = [region[pl.ds(low + TILE, TILE), hcols] for low in key_lows]
            scores = [
                jnp.where(live[b], nt(query, keys[b]) * score_scale, -jnp.inf) for b in range(BLOCKS)
            ]
            top = jnp.max(jnp.maximum(jnp.maximum(scores[0], scores[1]), scores[2]), -1, keepdims=True)
            exps = [jnp.exp(s - top) for s in scores]
            norm = jnp.sum(exps[0] + exps[1] + exps[2], -1, keepdims=True)
            inverse = 1.0 / norm
            probs = [e * inverse for e in exps]
            weights = [p.astype(jnp.bfloat16) for p in probs]
            attended = nn(weights[0], values[0]) + nn(weights[1], values[1]) + nn(weights[2], values[2])
            attended = attended.astype(jnp.bfloat16)
            attended_ref[rows, hcols] = attended
            delta = jnp.sum(grad.astype(jnp.float32) * attended.astype(jnp.float32), -1, keepdims=True)
            grad_scores = [
                (probs[b] * (nt(grad, values[b]) - delta)).astype(jnp.bfloat16) for b in range(BLOCKS)
            ]
            query_grad = (
                nn(grad_scores[0], keys[0]) + nn(grad_scores[1], keys[1]) + nn(grad_scores[2], keys[2])
            )
            query_grad_ref[rows, hcols] = (query_grad * score_scale).astype(query_grad_ref.dtype)
            for b in range(BLOCKS):
                at_key, at_value = pl.ds(key_lows[b], TILE), pl.ds(key_lows[b] + TILE, TILE)
                sums[at_key, hcols] += tn(grad_scores[b], query) * score_scale
                sums[at_value, hcols] += tn(weights[b], grad)
    for n in range(SPAN):
        term_refs[n][...] = sums[pl.ds(n * 2 * TILE, 2 * TILE), :].astype(term_refs[n].dtype)


def vm():
    return pl.BlockSpec(memory_space=VMEM)


def sm():
    return pl.BlockSpec(memory_space=SMEM)


def step(queries, keys, values, out_weight, out_grad, align_lists, block_masks):
    slabs = lax.axis_size("tm")
    groups = lax.axis_size("head")
    chips = groups // 2
    slab = jnp.full((1,), lax.axis_index("tm"), jnp.int32)
    group = jnp.full((1,), lax.axis_index("head"), jnp.int32)
    rows, cols = queries.shape
    bf16, f32 = jnp.bfloat16, jnp.float32

    def along(x, by):
        return lax.ppermute(x, "tm", [(t, (t + by) % slabs) for t in range(slabs)])

    def across(x, by0, by1):
        pairs = [
            (2 * c + k, 2 * ((c + (by1 if k else by0)) % chips) + k)
            for c in range(chips)
            for k in range(2)
        ]
        return lax.ppermute(x, "head", pairs)

    def swap(x):
        return lax.ppermute(x, "head", [(g, g ^ 1) for g in range(groups)])

    def kernel(body, args, in_specs, outs, scratch=(), flops=0, limit=None, exps=0):
        moved = sum(math.prod(a.shape) * a.dtype.itemsize for a in (*args, *outs))
        return pl.pallas_call(
            body,
            out_shape=outs,
            in_specs=in_specs,
            out_specs=[vm()] * len(outs),
            scratch_shapes=list(scratch),
            compiler_params=pltpu.CompilerParams(vmem_limit_bytes=limit),
            cost_estimate=pl.CostEstimate(flops=flops, bytes_accessed=moved, transcendentals=exps),
        )(*args)

    block = jax.ShapeDtypeStruct((rows, cols), bf16)
    own = jnp.concatenate([keys, values], 0)
    a_block = across(out_grad, 1, -1)
    r1 = along(own, 1)
    b_block = across(out_grad, -1, 1)
    l1 = along(own, -1)
    c_block = across(a_block, 1, -1)
    r2 = along(r1, 1)
    l2 = along(l1, -1)
    mine = jnp.concatenate([out_grad, a_block, b_block, c_block], 0)
    theirs = swap(mine)
    r3 = along(r2, 1)
    l3 = along(l2, -1)

    (grad_attended,) = kernel(
        functools.partial(grad_attended_kernel, chips),
        (group, mine, theirs, out_weight),
        [sm(), vm(), vm(), vm()],
        [block],
        flops=2 * rows * cols * groups * cols,
        limit=LIMIT,
    )
    outs = kernel(
        attention_kernel,
        (slab, align_lists.T, block_masks, queries, grad_attended, r3, r2, r1, own, l1, l2, l3),
        [sm()] * 3 + [vm()] * (2 + SPAN),
        [block] * (2 + REACH) + [jax.ShapeDtypeStruct(own.shape, f32)] + [block] * REACH,
        scratch=(VMEM((SPAN * 2 * TILE, cols), bf16), VMEM((SPAN * 2 * TILE, cols), f32)),
        flops=14 * rows * cols * BLOCKS * TILE,
        exps=rows * cols * BLOCKS,
        limit=LIMIT,
    )
    attended, query_grad = outs[:2]
    terms = outs[2:]
    send, keep = kernel(
        functools.partial(out_proj_kernel, chips),
        (group, attended, out_weight),
        [sm(), vm(), vm()],
        [jax.ShapeDtypeStruct((4 * rows, cols), bf16)] * 2,
        flops=2 * rows * cols * groups * cols,
        limit=LIMIT,
    )

    def add(x, y):
        return (x.astype(f32) + y.astype(f32)).astype(bf16)

    rightward, leftward = terms[2 * REACH], terms[0]
    for n in range(REACH, 0, -1):
        rightward = along(rightward, 1)
        leftward = along(leftward, -1)
        if n > 1:
            rightward = add(rightward, terms[REACH + n - 1])
            leftward = add(leftward, terms[REACH - n + 1])
    pair_sums = add(keep, swap(send)).reshape(4, rows, cols)
    arrived = [across(pair_sums[s], s, s) for s in (1, 3, 2)]
    total = terms[REACH] + rightward.astype(f32) + leftward.astype(f32)
    key_grad = total[:TILE].astype(bf16)
    value_grad = total[TILE:].astype(bf16)
    mixed = pair_sums[0].astype(f32)
    for part in arrived:
        mixed = mixed + part.astype(f32)
    return (mixed.astype(bf16), query_grad, key_grad, value_grad)


def solution(mesh):
    return jax.shard_map(
        step,
        mesh=mesh,
        in_specs=(
            P("tm", "head"),
            P("tm", "head"),
            P("tm", "head"),
            P("head", None),
            P("tm", "head"),
            P(),
            P("tm", None),
        ),
        out_specs=(P("tm", "head"), P("tm", "head"), P("tm", "head"), P("tm", "head")),
        check_vma=False,
    )
```

time: 136 us -> 131 us (0.963)
  Pallas kernels: 15.3 us -> 8.31 us
  waiting for transfers between devices: 25.4 us -> 29 us
  local copies, waits for them, and re-layouts: 5.44 us -> 3.52 us
    pallas_call x3, Pallas kernels: 15.3 us -> 8.31 us  [kernel(): pl.pallas_call(body, out_shape=outs, in_specs=in_specs, out_specs=[vm()]...]
    ppermute x12, waiting for transfers between devices: 14.3 us -> 17.9 us  [along(): return lax.ppermute(x, 'tm', [(t, (t + by) % slabs) for t in range(slabs)])]
    unnamed x41 -> x18, local copies, waits for them, and re-layouts: 3.32 us -> 2.72 us
  transfers between devices with their start and end apart: 20 -> 20, of which waited for: 12 -> 12; matrix products, arithmetic and copies ran while one was open for 3% -> 2% of each run, Pallas kernels for 6% -> 2%
where the time goes in v2:
time: 131 us; the launch traced here: 130 us
  starting transfers between devices  86.7 us (66%)
  waiting for transfers between devices  29 us (22%)
  Pallas kernels  8.31 us (6%)
  local copies, waits for them, and re-layouts  3.52 us (3%)
    ppermute x12, starting transfers between devices, along(): return lax.ppermute(x, 'tm', [(t, (t + by) % slabs) for t in range(slabs)])  58.7 us
    ppermute x6, starting transfers between devices, across(): return lax.ppermute(x, 'head', pairs)  24.2 us
    ppermute x12, waiting for transfers between devices, along(): return lax.ppermute(x, 'tm', [(t, (t + by) % slabs) for t in range(slabs)])  17.9 us
    ppermute x6, waiting for transfers between devices, across(): return lax.ppermute(x, 'head', pairs)  11 us
    pallas_call x3, Pallas kernels, kernel(): pl.pallas_call(body, out_shape=outs, in_specs=in_specs, out_specs=[vm()]...  8.31 us
    ppermute x2, starting transfers between devices, swap(): return lax.ppermute(x, 'head', [(g, g ^ 1) for g in range(groups)])  3.84 us
    unnamed x18, local copies, waits for them, and re-layouts  2.72 us
  transfers between devices with their start and end apart: 20, of which 12 were waited for; matrix products, arithmetic and copies ran while one was open for 2% of the time, Pallas kernels for 2%

profile of v2, /device:TPU:6, one launch (start us, length us, event | category | flops | bytes accessed | tf_op | source)
XLA Modules:
  0.0 129.8 jit_solution(3586553906383453893)
XLA Ops:
  0.7 7.9 %collective-permute-start = (bf16[256,384]{1,0:T(8,128)(2,1)}, bf16[256,384]{1,0:T(8,128)(2,1)S(1)}, u32[]{:S(2)}, u32[]{:S(2)}) collective-permute-start(bf16[256,384]{1,0:T(8,128)(2,1)} %param.11), channel_id=1, source_target_pairs={{0,2},{1,7},{2,4},{3,1},{4,6},{5,3},{6,0},{7,5},{8,10},{9,15},{10,... | collective-permute-start | bytes 589832 | tf_op jit(solution)/shard_map/ppermute | solution.py:144
  12.0 5.5 %collective-permute-start.2 = (bf16[256,384]{1,0:T(8,128)(2,1)S(1)}, bf16[256,384]{1,0:T(8,128)(2,1)S(1)}, u32[]{:S(2)}, u32[]{:S(2)}) collective-permute-start(bf16[256,384]{1,0:T(8,128)(2,1)S(1)} %collective-permute-done), channel_id=1, source_target_pairs={{0,2},{1,7},{2,4},{3,1},{4,6},{5,3},{6,0},{7,5},{8,10},{9,15},{10,... | collective-permute-start | bytes 589832 | tf_op jit(solution)/shard_map/ppermute | solution.py:144
  18.4 2.3 %collective-permute-done.2 = bf16[256,384]{1,0:T(8,128)(2,1)S(1)} collective-permute-done((bf16[256,384]{1,0:T(8,128)(2,1)S(1)}, bf16[256,384]{1,0:T(8,128)(2,1)S(1)}, u32[]{:S(2)}, u32[]{:S(2)}) %collective-permute-start.2) | collective-permute-done | bytes 196640 | tf_op jit(solution)/shard_map/ppermute | solution.py:144
  20.7 1.9 %collective-permute-start.3 = (bf16[1024,384]{1,0:T(8,128)(2,1)S(1)}, bf16[1024,384]{1,0:T(8,128)(2,1)S(1)}, u32[]{:S(2)}, u32[]{:S(2)}) collective-permute-start(bf16[1024,384]{1,0:T(8,128)(2,1)S(1)} %constant_dynamic-update-slice_fusion.mine_ref), channel_id=1, source_target_pairs={{0,1},{1,0},{2,3},{3,2},{4,5},{5,4},{6,7},{7,6},{8,9},{9,8},{10,11... | collective-permute-start | bytes 2359304 | tf_op jit(solution)/shard_map/ppermute | solution.py:147
  22.7 10.1 %collective-permute-start.7 = (bf16[256,384]{1,0:T(8,128)(2,1)S(1)}, bf16[256,384]{1,0:T(8,128)(2,1)S(1)}, u32[]{:S(2)}, u32[]{:S(2)}) collective-permute-start(bf16[256,384]{1,0:T(8,128)(2,1)S(1)} %constant_dynamic-update-slice_fusion.4.refs_3_), channel_id=1, source_target_pairs={{0,504},{8,0},{16,8},{24,16},{32,24},{40,32},{48,40},{56,48},{64,5... | collective-permute-start | bytes 589832 | tf_op jit(solution)/shard_map/ppermute | solution.py:136
  32.8 1.9 %collective-permute-start.4 = (bf16[256,384]{1,0:T(8,128)(2,1)S(1)}, bf16[256,384]{1,0:T(8,128)(2,1)S(1)}, u32[]{:S(2)}, u32[]{:S(2)}) collective-permute-start(bf16[256,384]{1,0:T(8,128)(2,1)S(1)} %constant_dynamic-update-slice_fusion.4.refs_3_), channel_id=1, source_target_pairs={{0,8},{8,16},{16,24},{24,32},{32,40},{40,48},{48,56},{56,64},{64,7... | collective-permute-start | bytes 589832 | tf_op jit(solution)/shard_map/ppermute | solution.py:136
  34.7 2.9 %collective-permute-done.7.refs_4_ = bf16[256,384]{1,0:T(8,128)(2,1)S(1)} collective-permute-done((bf16[256,384]{1,0:T(8,128)(2,1)S(1)}, bf16[256,384]{1,0:T(8,128)(2,1)S(1)}, u32[]{:S(2)}, u32[]{:S(2)}) %collective-permute-start.7) | collective-permute-done | bytes 196640 | tf_op jit(solution)/shard_map/ppermute | solution.py:136
  37.6 7.7 %collective-permute-start.8 = (bf16[256,384]{1,0:T(8,128)(2,1)S(1)}, bf16[256,384]{1,0:T(8,128)(2,1)S(1)}, u32[]{:S(2)}, u32[]{:S(2)}) collective-permute-start(bf16[256,384]{1,0:T(8,128)(2,1)S(1)} %collective-permute-done.7.refs_4_), channel_id=1, source_target_pairs={{0,504},{8,0},{16,8},{24,16},{32,24},{40,32},{48,40},{56,48},{64,5... | collective-permute-start | bytes 589832 | tf_op jit(solution)/shard_map/ppermute | solution.py:136
  45.3 1.9 %collective-permute-start.5 = (bf16[256,384]{1,0:T(8,128)(2,1)S(1)}, bf16[256,384]{1,0:T(8,128)(2,1)S(1)}, u32[]{:S(2)}, u32[]{:S(2)}) collective-permute-start(bf16[256,384]{1,0:T(8,128)(2,1)S(1)} %collective-permute-done.4.refs_2_), channel_id=1, source_target_pairs={{0,8},{8,16},{16,24},{24,32},{32,40},{40,48},{48,56},{56,64},{64,7... | collective-permute-start | bytes 589832 | tf_op jit(solution)/shard_map/ppermute | solution.py:136
  47.2 2.0 %collective-permute-done.8.refs_5_ = bf16[256,384]{1,0:T(8,128)(2,1)S(1)} collective-permute-done((bf16[256,384]{1,0:T(8,128)(2,1)S(1)}, bf16[256,384]{1,0:T(8,128)(2,1)S(1)}, u32[]{:S(2)}, u32[]{:S(2)}) %collective-permute-start.8) | collective-permute-done | bytes 196640 | tf_op jit(solution)/shard_map/ppermute | solution.py:136
  49.2 7.7 %collective-permute-start.9 = (bf16[256,384]{1,0:T(8,128)(2,1)S(1)}, bf16[256,384]{1,0:T(8,128)(2,1)S(1)}, u32[]{:S(2)}, u32[]{:S(2)}) collective-permute-start(bf16[256,384]{1,0:T(8,128)(2,1)S(1)} %collective-permute-done.8.refs_5_), channel_id=1, source_target_pairs={{0,504},{8,0},{16,8},{24,16},{32,24},{40,32},{48,40},{56,48},{64,5... | collective-permute-start | bytes 589832 | tf_op jit(solution)/shard_map/ppermute | solution.py:136
  56.9 1.9 %collective-permute-start.6 = (bf16[256,384]{1,0:T(8,128)(2,1)S(1)}, bf16[256,384]{1,0:T(8,128)(2,1)S(1)}, u32[]{:S(2)}, u32[]{:S(2)}) collective-permute-start(bf16[256,384]{1,0:T(8,128)(2,1)S(1)} %collective-permute-done.5.refs_1_), channel_id=1, source_target_pairs={{0,8},{8,16},{16,24},{24,32},{32,40},{40,48},{48,56},{56,64},{64,7... | collective-permute-start | bytes 589832 | tf_op jit(solution)/shard_map/ppermute | solution.py:136
  61.7 6.1 %collective-permute-done.6.refs_0_ = bf16[256,384]{1,0:T(8,128)(2,1)S(1)} collective-permute-done((bf16[256,384]{1,0:T(8,128)(2,1)S(1)}, bf16[256,384]{1,0:T(8,128)(2,1)S(1)}, u32[]{:S(2)}, u32[]{:S(2)}) %collective-permute-start.6) | collective-permute-done | bytes 196640 | tf_op jit(solution)/shard_map/ppermute | solution.py:136
  67.8 6.0 %shard_map.103 = (bf16[256,384]{1,0:T(8,128)(2,1)S(1)}, bf16[256,384]{1,0:T(8,128)(2,1)}, bf16[256,384]{1,0:T(8,128)(2,1)S(1)}, bf16[256,384]{1,0:T(8,128)(2,1)S...) custom-call(s32[1]{0:T(128)} %bitcast.1.slab_ref, ...), custom_call_target="tpu_custom_call" | custom-call | flops 528482304 | bytes 3736604 | tf_op jit(solution)/shard_map/pallas_call | solution.py:151
  75.8 7.2 %collective-permute-start.17 = (bf16[256,384]{1,0:T(8,128)(2,1)S(1)}, bf16[256,384]{1,0:T(8,128)(2,1)S(1)}, u32[]{:S(2)}, u32[]{:S(2)}) collective-permute-start(bf16[256,384]{1,0:T(8,128)(2,1)S(1)} %get-tuple-element.23), channel_id=1, source_target_pairs={{0,504},{8,0},{16,8},{24,16},{32,24},{40,32},{48,40},{56,48},{64,5... | collective-permute-start | bytes 589832 | tf_op jit(solution)/shard_map/ppermute | solution.py:136
  84.2 1.9 %collective-permute-start.10 = (bf16[1024,384]{1,0:T(8,128)(2,1)S(1)}, bf16[1024,384]{1,0:T(8,128)(2,1)S(1)}, u32[]{:S(2)}, u32[]{:S(2)}) collective-permute-start(bf16[1024,384]{1,0:T(8,128)(2,1)S(1)} %get-tuple-element.17), channel_id=1, source_target_pairs={{0,1},{1,0},{2,3},{3,2},{4,5},{5,4},{6,7},{7,6},{8,9},{9,8},{10,11... | collective-permute-start | bytes 2359304 | tf_op jit(solution)/shard_map/ppermute | solution.py:147
  88.2 7.2 %collective-permute-start.18 = (bf16[256,384]{1,0:T(8,128)(2,1)S(1)}, bf16[256,384]{1,0:T(8,128)(2,1)S(1)}, u32[]{:S(2)}, u32[]{:S(2)}) collective-permute-start(bf16[256,384]{1,0:T(8,128)(2,1)S(1)} %add_convert_fusion.3), channel_id=1, source_target_pairs={{0,504},{8,0},{16,8},{24,16},{32,24},{40,32},{48,40},{56,48},{64,5... | collective-permute-start | bytes 589832 | tf_op jit(solution)/shard_map/ppermute | solution.py:136
  95.4 3.3 %collective-permute-done.15 = bf16[256,384]{1,0:T(8,128)(2,1)S(1)} collective-permute-done((bf16[256,384]{1,0:T(8,128)(2,1)S(1)}, bf16[256,384]{1,0:T(8,128)(2,1)S(1)}, u32[]{:S(2)}, u32[]{:S(2)}) %collective-permute-start.15) | collective-permute-done | bytes 196640 | tf_op jit(solution)/shard_map/ppermute | solution.py:136
  100.7 7.2 %collective-permute-start.19 = (bf16[256,384]{1,0:T(8,128)(2,1)S(1)}, bf16[256,384]{1,0:T(8,128)(2,1)S(1)}, u32[]{:S(2)}, u32[]{:S(2)}) collective-permute-start(bf16[256,384]{1,0:T(8,128)(2,1)S(1)} %add_convert_fusion.2), channel_id=1, source_target_pairs={{0,504},{8,0},{16,8},{24,16},{32,24},{40,32},{48,40},{56,48},{64,5... | collective-permute-start | bytes 589832 | tf_op jit(solution)/shard_map/ppermute | solution.py:136
  108.0 2.4 %collective-permute-done.16 = bf16[256,384]{1,0:T(8,128)(2,1)S(1)} collective-permute-done((bf16[256,384]{1,0:T(8,128)(2,1)S(1)}, bf16[256,384]{1,0:T(8,128)(2,1)S(1)}, u32[]{:S(2)}, u32[]{:S(2)}) %collective-permute-start.16) | collective-permute-done | bytes 196640 | tf_op jit(solution)/shard_map/ppermute | solution.py:136
  112.0 4.0 %collective-permute-start.11 = (bf16[256,384]{1,0:T(8,128)(2,1)S(1)}, bf16[256,384]{1,0:T(8,128)(2,1)S(1)}, u32[]{:S(2)}, u32[]{:S(2)}) collective-permute-start(bf16[256,384]{1,0:T(8,128)(2,1)S(1)} %get-tuple-element.26), channel_id=1, source_target_pairs={{0,2},{1,3},{2,4},{3,5},{4,6},{5,7},{6,0},{7,1},{8,10},{9,11},{10,... | collective-permute-start | bytes 589832 | tf_op jit(solution)/shard_map/ppermute | solution.py:144
  116.1 3.0 %collective-permute-start.13 = (bf16[256,384]{1,0:T(8,128)(2,1)S(1)}, bf16[256,384]{1,0:T(8,128)(2,1)S(1)}, u32[]{:S(2)}, u32[]{:S(2)}) collective-permute-start(bf16[256,384]{1,0:T(8,128)(2,1)S(1)} %get-tuple-element.27), channel_id=1, source_target_pairs={{0,4},{1,5},{2,6},{3,7},{4,0},{5,1},{6,2},{7,3},{8,12},{9,13},{10,... | collective-permute-start | bytes 589832 | tf_op jit(solution)/shard_map/ppermute | solution.py:144
  123.4 3.4 %collective-permute-done.13 = bf16[256,384]{1,0:T(8,128)(2,1)S(1)} collective-permute-done((bf16[256,384]{1,0:T(8,128)(2,1)S(1)}, bf16[256,384]{1,0:T(8,128)(2,1)S(1)}, u32[]{:S(2)}, u32[]{:S(2)}) %collective-permute-start.13) | collective-permute-done | bytes 196640 | tf_op jit(solution)/shard_map/ppermute | solution.py:144
  126.7 2.3 %collective-permute-done.12 = bf16[256,384]{1,0:T(8,128)(2,1)S(1)} collective-permute-done((bf16[256,384]{1,0:T(8,128)(2,1)S(1)}, bf16[256,384]{1,0:T(8,128)(2,1)S(1)}, u32[]{:S(2)}, u32[]{:S(2)}) %collective-permute-start.12) | collective-permute-done | bytes 196640 | tf_op jit(solution)/shard_map/ppermute | solution.py:144
  (48 shorter events, 21.0 us)
Async XLA Ops:
  0.6 22.0 %copy-start.5 = (bf16[128,384]{1,0:T(8,128)(2,1)S(1)}, bf16[128,384]{1,0:T(8,128)(2,1)}, u32[]{:S(2)}) copy-start(bf16[128,384]{1,0:T(8,128)(2,1)} %param.8) | copy-start | bytes 294916
  0.6 22.0 %copy-start.6 = (bf16[128,384]{1,0:T(8,128)(2,1)S(1)}, bf16[128,384]{1,0:T(8,128)(2,1)}, u32[]{:S(2)}) copy-start(bf16[128,384]{1,0:T(8,128)(2,1)} %param.9) | copy-start | bytes 294916
  0.7 11.4 %collective-permute-start = (bf16[256,384]{1,0:T(8,128)(2,1)}, bf16[256,384]{1,0:T(8,128)(2,1)S(1)}, u32[]{:S(2)}, u32[]{:S(2)}) collective-permute-start(bf16[256,384]{1,0:T(8,128)(2,1)} %param.11), channel_id=1, source_target_pairs={{0,2},{1,7},{2,4},{3,1},{4,6},{5,3},{6,0},{7,5},{8,10},{9,15},{10,... | collective-permute-start | bytes 589832 | tf_op jit(solution)/shard_map/ppermute | solution.py:144
  8.5 9.8 %collective-permute-start.1 = (bf16[256,384]{1,0:T(8,128)(2,1)}, bf16[256,384]{1,0:T(8,128)(2,1)S(1)}, u32[]{:S(2)}, u32[]{:S(2)}) collective-permute-start(bf16[256,384]{1,0:T(8,128)(2,1)} %param.11), channel_id=1, source_target_pairs={{0,6},{1,3},{2,0},{3,5},{4,2},{5,7},{6,4},{7,1},{8,14},{9,11},{10,... | collective-permute-start | bytes 589832 | tf_op jit(solution)/shard_map/ppermute | solution.py:144
  12.0 8.7 %collective-permute-start.2 = (bf16[256,384]{1,0:T(8,128)(2,1)S(1)}, bf16[256,384]{1,0:T(8,128)(2,1)S(1)}, u32[]{:S(2)}, u32[]{:S(2)}) collective-permute-start(bf16[256,384]{1,0:T(8,128)(2,1)S(1)} %collective-permute-done), channel_id=1, source_target_pairs={{0,2},{1,7},{2,4},{3,1},{4,6},{5,3},{6,0},{7,5},{8,10},{9,15},{10,... | collective-permute-start | bytes 589832 | tf_op jit(solution)/shard_map/ppermute | solution.py:144
  20.7 38.2 %collective-permute-start.3 = (bf16[1024,384]{1,0:T(8,128)(2,1)S(1)}, bf16[1024,384]{1,0:T(8,128)(2,1)S(1)}, u32[]{:S(2)}, u32[]{:S(2)}) collective-permute-start(bf16[1024,384]{1,0:T(8,128)(2,1)S(1)} %constant_dynamic-update-slice_fusion.mine_ref), channel_id=1, source_target_pairs={{0,1},{1,0},{2,3},{3,2},{4,5},{5,4},{6,7},{7,6},{8,9},{9,8},{10,11... | collective-permute-start | bytes 2359304 | tf_op jit(solution)/shard_map/ppermute | solution.py:147
  22.7 14.9 %collective-permute-start.7 = (bf16[256,384]{1,0:T(8,128)(2,1)S(1)}, bf16[256,384]{1,0:T(8,128)(2,1)S(1)}, u32[]{:S(2)}, u32[]{:S(2)}) collective-permute-start(bf16[256,384]{1,0:T(8,128)(2,1)S(1)} %constant_dynamic-update-slice_fusion.4.refs_3_), channel_id=1, source_target_pairs={{0,504},{8,0},{16,8},{24,16},{32,24},{40,32},{48,40},{56,48},{64,5... | collective-permute-start | bytes 589832 | tf_op jit(solution)/shard_map/ppermute | solution.py:136
  32.8 12.5 %collective-permute-start.4 = (bf16[256,384]{1,0:T(8,128)(2,1)S(1)}, bf16[256,384]{1,0:T(8,128)(2,1)S(1)}, u32[]{:S(2)}, u32[]{:S(2)}) collective-permute-start(bf16[256,384]{1,0:T(8,128)(2,1)S(1)} %constant_dynamic-update-slice_fusion.4.refs_3_), channel_id=1, source_target_pairs={{0,8},{8,16},{16,24},{24,32},{32,40},{40,48},{48,56},{56,64},{64,7... | collective-permute-start | bytes 589832 | tf_op jit(solution)/shard_map/ppermute | solution.py:136
  37.6 11.6 %collective-permute-start.8 = (bf16[256,384]{1,0:T(8,128)(2,1)S(1)}, bf16[256,384]{1,0:T(8,128)(2,1)S(1)}, u32[]{:S(2)}, u32[]{:S(2)}) collective-permute-start(bf16[256,384]{1,0:T(8,128)(2,1)S(1)} %collective-permute-done.7.refs_4_), channel_id=1, source_target_pairs={{0,504},{8,0},{16,8},{24,16},{32,24},{40,32},{48,40},{56,48},{64,5... | collective-permute-start | bytes 589832 | tf_op jit(solution)/shard_map/ppermute | solution.py:136
  45.3 11.6 %collective-permute-start.5 = (bf16[256,384]{1,0:T(8,128)(2,1)S(1)}, bf16[256,384]{1,0:T(8,128)(2,1)S(1)}, u32[]{:S(2)}, u32[]{:S(2)}) collective-permute-start(bf16[256,384]{1,0:T(8,128)(2,1)S(1)} %collective-permute-done.4.refs_2_), channel_id=1, source_target_pairs={{0,8},{8,16},{16,24},{24,32},{32,40},{40,48},{48,56},{56,64},{64,7... | collective-permute-start | bytes 589832 | tf_op jit(solution)/shard_map/ppermute | solution.py:136
  49.2 12.5 %collective-permute-start.9 = (bf16[256,384]{1,0:T(8,128)(2,1)S(1)}, bf16[256,384]{1,0:T(8,128)(2,1)S(1)}, u32[]{:S(2)}, u32[]{:S(2)}) collective-permute-start(bf16[256,384]{1,0:T(8,128)(2,1)S(1)} %collective-permute-done.8.refs_5_), channel_id=1, source_target_pairs={{0,504},{8,0},{16,8},{24,16},{32,24},{40,32},{48,40},{56,48},{64,5... | collective-permute-start | bytes 589832 | tf_op jit(solution)/shard_map/ppermute | solution.py:136
  56.9 10.9 %collective-permute-start.6 = (bf16[256,384]{1,0:T(8,128)(2,1)S(1)}, bf16[256,384]{1,0:T(8,128)(2,1)S(1)}, u32[]{:S(2)}, u32[]{:S(2)}) collective-permute-start(bf16[256,384]{1,0:T(8,128)(2,1)S(1)} %collective-permute-done.5.refs_1_), channel_id=1, source_target_pairs={{0,8},{8,16},{16,24},{24,32},{32,40},{40,48},{48,56},{56,64},{64,7... | collective-permute-start | bytes 589832 | tf_op jit(solution)/shard_map/ppermute | solution.py:136
  60.6 7.3 %copy-start.4 = (s32[2,3]{1,0:T(2,128)S(1)}, s32[2,3]{1,0:T(2,128)}, u32[]{:S(2)}) copy-start(s32[2,3]{1,0:T(2,128)} %mask_ref.1) | copy-start | bytes 76
  60.6 22.5 %copy-start.1 = (bf16[384,3072]{1,0:T(8,128)(2,1)S(1)}, bf16[384,3072]{1,0:T(8,128)(2,1)}, u32[]{:S(2)}) copy-start(bf16[384,3072]{1,0:T(8,128)(2,1)} %weight_ref.3) | copy-start | bytes 7077892
  73.9 12.2 %collective-permute-start.14 = (bf16[256,384]{1,0:T(8,128)(2,1)S(1)}, bf16[256,384]{1,0:T(8,128)(2,1)S(1)}, u32[]{:S(2)}, u32[]{:S(2)}) collective-permute-start(bf16[256,384]{1,0:T(8,128)(2,1)S(1)} %get-tuple-element.20), channel_id=1, source_target_pairs={{0,8},{8,16},{16,24},{24,32},{32,40},{40,48},{48,56},{56,64},{64,7... | collective-permute-start | bytes 589832 | tf_op jit(solution)/shard_map/ppermute | solution.py:136
  75.8 12.3 %collective-permute-start.17 = (bf16[256,384]{1,0:T(8,128)(2,1)S(1)}, bf16[256,384]{1,0:T(8,128)(2,1)S(1)}, u32[]{:S(2)}, u32[]{:S(2)}) collective-permute-start(bf16[256,384]{1,0:T(8,128)(2,1)S(1)} %get-tuple-element.23), channel_id=1, source_target_pairs={{0,504},{8,0},{16,8},{24,16},{32,24},{40,32},{48,40},{56,48},{64,5... | collective-permute-start | bytes 589832 | tf_op jit(solution)/shard_map/ppermute | solution.py:136
  84.2 27.6 %collective-permute-start.10 = (bf16[1024,384]{1,0:T(8,128)(2,1)S(1)}, bf16[1024,384]{1,0:T(8,128)(2,1)S(1)}, u32[]{:S(2)}, u32[]{:S(2)}) collective-permute-start(bf16[1024,384]{1,0:T(8,128)(2,1)S(1)} %get-tuple-element.17), channel_id=1, source_target_pairs={{0,1},{1,0},{2,3},{3,2},{4,5},{5,4},{6,7},{7,6},{8,9},{9,8},{10,11... | collective-permute-start | bytes 2359304 | tf_op jit(solution)/shard_map/ppermute | solution.py:147
  86.2 12.5 %collective-permute-start.15 = (bf16[256,384]{1,0:T(8,128)(2,1)S(1)}, bf16[256,384]{1,0:T(8,128)(2,1)S(1)}, u32[]{:S(2)}, u32[]{:S(2)}) collective-permute-start(bf16[256,384]{1,0:T(8,128)(2,1)S(1)} %add_convert_fusion.5), channel_id=1, source_target_pairs={{0,8},{8,16},{16,24},{24,32},{32,40},{40,48},{48,56},{56,64},{64,7... | collective-permute-start | bytes 589832 | tf_op jit(solution)/shard_map/ppermute | solution.py:136
  88.2 12.5 %collective-permute-start.18 = (bf16[256,384]{1,0:T(8,128)(2,1)S(1)}, bf16[256,384]{1,0:T(8,128)(2,1)S(1)}, u32[]{:S(2)}, u32[]{:S(2)}) collective-permute-start(bf16[256,384]{1,0:T(8,128)(2,1)S(1)} %add_convert_fusion.3), channel_id=1, source_target_pairs={{0,504},{8,0},{16,8},{24,16},{32,24},{40,32},{48,40},{56,48},{64,5... | collective-permute-start | bytes 589832 | tf_op jit(solution)/shard_map/ppermute | solution.py:136
  98.7 11.7 %collective-permute-start.16 = (bf16[256,384]{1,0:T(8,128)(2,1)S(1)}, bf16[256,384]{1,0:T(8,128)(2,1)S(1)}, u32[]{:S(2)}, u32[]{:S(2)}) collective-permute-start(bf16[256,384]{1,0:T(8,128)(2,1)S(1)} %add_convert_fusion.4), channel_id=1, source_target_pairs={{0,8},{8,16},{16,24},{24,32},{32,40},{40,48},{48,56},{56,64},{64,7... | collective-permute-start | bytes 589832 | tf_op jit(solution)/shard_map/ppermute | solution.py:136
  100.7 10.9 %collective-permute-start.19 = (bf16[256,384]{1,0:T(8,128)(2,1)S(1)}, bf16[256,384]{1,0:T(8,128)(2,1)S(1)}, u32[]{:S(2)}, u32[]{:S(2)}) collective-permute-start(bf16[256,384]{1,0:T(8,128)(2,1)S(1)} %add_convert_fusion.2), channel_id=1, source_target_pairs={{0,504},{8,0},{16,8},{24,16},{32,24},{40,32},{48,40},{56,48},{64,5... | collective-permute-start | bytes 589832 | tf_op jit(solution)/shard_map/ppermute | solution.py:136
  112.0 11.3 %collective-permute-start.11 = (bf16[256,384]{1,0:T(8,128)(2,1)S(1)}, bf16[256,384]{1,0:T(8,128)(2,1)S(1)}, u32[]{:S(2)}, u32[]{:S(2)}) collective-permute-start(bf16[256,384]{1,0:T(8,128)(2,1)S(1)} %get-tuple-element.26), channel_id=1, source_target_pairs={{0,2},{1,3},{2,4},{3,5},{4,6},{5,7},{6,0},{7,1},{8,10},{9,11},{10,... | collective-permute-start | bytes 589832 | tf_op jit(solution)/shard_map/ppermute | solution.py:144
  116.1 10.7 %collective-permute-start.13 = (bf16[256,384]{1,0:T(8,128)(2,1)S(1)}, bf16[256,384]{1,0:T(8,128)(2,1)S(1)}, u32[]{:S(2)}, u32[]{:S(2)}) collective-permute-start(bf16[256,384]{1,0:T(8,128)(2,1)S(1)} %get-tuple-element.27), channel_id=1, source_target_pairs={{0,4},{1,5},{2,6},{3,7},{4,0},{5,1},{6,2},{7,3},{8,12},{9,13},{10,... | collective-permute-start | bytes 589832 | tf_op jit(solution)/shard_map/ppermute | solution.py:144
  119.1 10.0 %collective-permute-start.12 = (bf16[256,384]{1,0:T(8,128)(2,1)S(1)}, bf16[256,384]{1,0:T(8,128)(2,1)S(1)}, u32[]{:S(2)}, u32[]{:S(2)}) collective-permute-start(bf16[256,384]{1,0:T(8,128)(2,1)S(1)} %get-tuple-element.28), channel_id=1, source_target_pairs={{0,6},{1,7},{2,0},{3,1},{4,2},{5,3},{6,4},{7,5},{8,14},{9,15},{10,... | collective-permute-start | bytes 589832 | tf_op jit(solution)/shard_map/ppermute | solution.py:144
  (3 other events, 16.2 us)
